TPU v7x, 128 devices: a whole 4x4x4 slice. The times are simulated.
128 devices in a mesh: pipe: 16 (over y, z_lo, core), fsdp: 8 (over z_hi, x).
Axes of the slice: x: 4, y: 4, z: 4 (z_hi: 2, z_lo: 2; z = z_hi * 2 + z_lo), core: 2. Of those that a mesh axis runs over, the one named last changes fastest.
Arguments:
- handoff_gradient: bfloat16 [16, 768, 8192], P('pipe', 'fsdp'), may hold values from -12 to 12
- output_weight: bfloat16 [16, 8192, 8192], P('pipe', 'fsdp'), may hold values from -0.0625 to 0.0625
- adapter_down: bfloat16 [16, 16, 8192], P('pipe', None, 'fsdp'), may hold values from -0.0625 to 0.0625
- adapter_up: bfloat16 [16, 16, 8192], P('pipe', None, 'fsdp'), may hold values from -0.29882812 to 0.29882812
- stored_queries: bfloat16 [16, 768, 8192], P('pipe', None, 'fsdp'), may hold values from -64 to 64
- stored_keys: bfloat16 [16, 768, 1024], P('pipe', None, 'fsdp'), may hold values from -3 to 3
- stored_values: bfloat16 [16, 768, 1024], P('pipe', None, 'fsdp'), may hold values from -6 to 6
- segments: int32 [16, 768], P('pipe'), may hold values from 0 to 7, never falling along the last dimension, each value on 1 to 384 neighbouring positions
Outputs:
- query_gradient: bfloat16 [16, 768, 8192], P('pipe', None, 'fsdp')
- key_gradient: bfloat16 [16, 768, 1024], P('pipe', None, 'fsdp')
- value_gradient: bfloat16 [16, 768, 1024], P('pipe', None, 'fsdp')
- down_map_gradient: float32 [16, 16, 8192], P('pipe', None, 'fsdp')
- up_map_gradient: float32 [16, 16, 8192], P('pipe', None, 'fsdp')
Inputs may be any that keep to these rules, and one draw needn't show every extreme that they name: `segments`: ids never fall along a micro-batch.
All inputs are finite; a program needn't handle non-finite values.
Results may differ from a plain program's by a relative error of at most 0.015.
The roundings to bfloat16 on the way count: a program that leaves them out, or rounds other values in their place, can miss the bound.
Values may be sent and summed in bfloat16 or wider, within the bound.
A program may use at most 128 MiB of HBM per device.

v0:
```python
import math

import jax
import jax.numpy as jnp
from jax import lax
from jax.sharding import PartitionSpec as P

HEAD_SIZE = 128


adapter_scale = 2.0


def swapped(block, axis, distance):
    count = lax.axis_size(axis)
    route = []
    for low in range(count):
        high = low | 1 << distance
        if high != low and high < count:
            route += [(low, high), (high, low)]
    return lax.ppermute(block, axis, route)


def shifted(block, axis, distance):
    devices = range(lax.axis_size(axis))
    route = [((i - distance) % len(devices), i) for i in devices]
    return lax.ppermute(block, axis, route)


def attend(query_block, key_head, value_head, context_gradient, allowed):
    inv_scale = 1.0 / math.sqrt(query_block.shape[-1])
    scores = (
        jnp.einsum("bngd,snd->ngbs", query_block, key_head, preferred_element_type=jnp.float32)
        * inv_scale
    )
    scores = jnp.where(allowed[None, None], scores, -jnp.inf)
    row_max = jnp.max(scores, axis=-1, keepdims=True)
    expanded = jnp.exp(scores - row_max)
    attn_probs = expanded / jnp.sum(expanded, axis=-1, keepdims=True)
    probs_low = attn_probs.astype(jnp.bfloat16)
    context_rows = jnp.einsum(
        "ngbs,snd->bngd", probs_low, value_head, preferred_element_type=jnp.float32
    )
    context_rows = lax.optimization_barrier(context_rows.astype(jnp.bfloat16))
    grad_probs = jnp.einsum(
        "bngd,snd->ngbs", context_gradient, value_head, preferred_element_type=jnp.float32
    )
    row_delta = jnp.sum(
        context_gradient.astype(jnp.float32) * context_rows.astype(jnp.float32), axis=-1
    )
    row_delta = jnp.transpose(row_delta, (1, 2, 0))[..., None]
    grad_scores = (attn_probs * (grad_probs - row_delta)).astype(jnp.bfloat16)
    grad_query = jnp.einsum(
        "ngbs,snd->bngd", grad_scores, key_head, preferred_element_type=jnp.float32
    )
    grad_query = (grad_query * inv_scale).astype(jnp.bfloat16)
    gradient_of_key = (
        jnp.einsum("ngbs,bngd->snd", grad_scores, query_block, preferred_element_type=jnp.float32)
        * inv_scale
    )
    gradient_of_value = jnp.einsum(
        "ngbs,bngd->snd", probs_low, context_gradient, preferred_element_type=jnp.float32
    )
    return (context_rows, grad_query, gradient_of_key, gradient_of_value)


def per_device(
    handoff_gradient,
    output_weight,
    adapter_down,
    adapter_up,
    stored_queries,
    stored_keys,
    stored_values,
    segments,
):
    pipe_count = lax.axis_size("pipe")
    member = lax.axis_index("fsdp")
    query_width = stored_queries.shape[2]
    kv_width = stored_keys.shape[2]
    packed = jnp.concatenate([stored_queries[0], stored_keys[0], stored_values[0]], axis=1)
    depth_levels = pipe_count.bit_length() - 1
    bit_order = list(range(depth_levels))
    for bit_index in bit_order:
        packed = swapped(packed, "pipe", bit_index)
    query = packed[:, :query_width]
    key_local = packed[:, query_width : query_width + kv_width]
    value_local = packed[:, query_width + kv_width :]
    sender_whole = lax.all_gather(handoff_gradient[0], "fsdp", axis=0, tiled=True)
    incoming_gradient = shifted(sender_whole, "pipe", -1)
    token_count = incoming_gradient.shape[0]
    local_width = adapter_up.shape[2]
    local_columns = lax.dynamic_slice_in_dim(
        incoming_gradient, member * local_width, local_width, 1
    )
    rank_portion = jnp.einsum(
        "yh,gh->yg", local_columns, adapter_up[0], preferred_element_type=jnp.float32
    )
    rank_gradient = lax.psum(rank_portion, "fsdp")
    frozen_portion = jnp.einsum(
        "td,qd->tq", incoming_gradient, output_weight[0], preferred_element_type=jnp.float32
    )
    rank_projected = jnp.dot(
        rank_gradient, adapter_down[0].astype(jnp.float32), precision=lax.Precision.HIGHEST
    )
    context_gradient = (frozen_portion + adapter_scale * rank_projected).astype(jnp.bfloat16)
    kv_heads = kv_width // HEAD_SIZE
    query_group_count = query_width // HEAD_SIZE // kv_heads
    query_shaped = query.reshape(token_count, kv_heads, query_group_count, HEAD_SIZE)
    grad_shaped = context_gradient.reshape(token_count, kv_heads, query_group_count, HEAD_SIZE)
    key_shaped = key_local.reshape(token_count, kv_heads, HEAD_SIZE)
    value_shaped = value_local.reshape(token_count, kv_heads, HEAD_SIZE)
    block_rows = math.gcd(token_count, 512)
    doc_ids = segments[0]
    positions = jnp.arange(token_count)

    def one_block(totals, block_index):
        row_start = block_index * block_rows
        query_block = lax.dynamic_slice_in_dim(query_shaped, row_start, block_rows, 0)
        grad_block = lax.dynamic_slice_in_dim(grad_shaped, row_start, block_rows, 0)
        row_ids = lax.dynamic_slice_in_dim(doc_ids, row_start, block_rows, 0)
        row_pos = row_start + jnp.arange(block_rows)
        allowed = (positions[None, :] <= row_pos[:, None]) & (row_ids[:, None] == doc_ids[None, :])
        context_rows, grad_query, gradient_of_key, gradient_of_value = attend(
            query_block, key_shaped, value_shaped, grad_block, allowed
        )
        return (
            (totals[0] + gradient_of_key, totals[1] + gradient_of_value),
            (context_rows, grad_query),
        )

    zero_kv = jnp.zeros((token_count, kv_heads, HEAD_SIZE), jnp.float32)
    (key_total, value_total), (contexts, grad_queries) = lax.scan(
        one_block, (zero_kv, zero_kv), jnp.arange(token_count // block_rows)
    )
    context_rows = contexts.reshape(token_count, query_width)
    query_gradient = grad_queries.reshape(token_count, query_width)
    key_gradient = key_total.reshape(token_count, kv_width).astype(jnp.bfloat16)
    value_gradient = value_total.reshape(token_count, kv_width).astype(jnp.bfloat16)
    context_portion = jnp.einsum(
        "yp,up->yu", context_rows, adapter_down[0], preferred_element_type=jnp.float32
    )
    rank_context = lax.psum(context_portion.astype(jnp.bfloat16), "fsdp").astype(jnp.float32)
    gradient_scale = adapter_scale / math.sqrt(token_count)
    down_map_gradient = gradient_scale * jnp.dot(
        rank_gradient.T, context_rows.astype(jnp.float32), precision=lax.Precision.HIGHEST
    )
    up_map_gradient = gradient_scale * jnp.dot(
        rank_context.T, local_columns.astype(jnp.float32), precision=lax.Precision.HIGHEST
    )
    return (
        query_gradient[None],
        key_gradient[None],
        value_gradient[None],
        down_map_gradient[None],
        up_map_gradient[None],
    )


def solution(mesh):
    placed = (
        P("pipe", "fsdp", None),
        P("pipe", "fsdp", None),
        P("pipe", None, "fsdp"),
        P("pipe", None, "fsdp"),
        P("pipe", None, "fsdp"),
        P("pipe", None, "fsdp"),
        P("pipe", None, "fsdp"),
        P("pipe", None),
    )
    return jax.shard_map(
        per_device,
        mesh=mesh,
        in_specs=placed,
        out_specs=(
            P("pipe", None, "fsdp"),
            P("pipe", None, "fsdp"),
            P("pipe", None, "fsdp"),
            P("pipe", None, "fsdp"),
            P("pipe", None, "fsdp"),
        ),
        check_vma=False,
    )
```

profile of v0, /device:TPU:0, one launch (start us, length us, event | category | flops | bytes accessed | tf_op | source)
XLA Modules:
  0.0 605.1 jit_solution(7616617631583650636)
XLA Ops:
  7.2 0.7 all-gather.3.cloned.1.call-update
  7.9 152.4 %all-gather.3.cloned.1.call-done = bf16[1,768,8192]{2,1,0:T(8,128)(2,1)} async-done(((bf16[1,96,8192]{2,1,0:T(8,128)(2,1)}), bf16[1,768,8192]{2,1,0:T(8,128)(2,1)}) %all-gather.3.cloned.1.call-update) | async-done | bytes 12582928 | tf_op jit(solution)/shard_map/all_gather | solution.py:89
  160.3 1.9 collective-permute-start.4
  162.2 1.1 copy.22
  163.2 1.7 copy.23
  165.0 0.7 copy.21
  165.7 1.1 pad_maximum_fusion
  166.8 15.4 %collective-permute-done = bf16[768,1280]{0,1:T(8,128)(2,1)S(1)} collective-permute-done((bf16[768,1280]{0,1:T(8,128)(2,1)S(1)}, bf16[768,1280]{0,1:T(8,128)(2,1)S(1)}, u32[]{:S(2)}, u32[]{:S(2)}) %collective-permute-start) | collective-permute-done | bytes 1966112 | tf_op jit(solution)/shard_map/ppermute | solution.py:21
  182.3 0.7 collective-permute-start.1
  182.9 157.1 %collective-permute-done.1 = bf16[768,1280]{0,1:T(8,128)(2,1)S(1)} collective-permute-done((bf16[768,1280]{0,1:T(8,128)(2,1)S(1)}, bf16[768,1280]{0,1:T(8,128)(2,1)S(1)}, u32[]{:S(2)}, u32[]{:S(2)}) %collective-permute-start.1) | collective-permute-done | bytes 1966112 | tf_op jit(solution)/shard_map/ppermute | solution.py:21
  340.1 1.5 collective-permute-start.2
  341.5 42.8 %collective-permute-done.2 = bf16[768,1280]{0,1:T(8,128)(2,1)} collective-permute-done((bf16[768,1280]{0,1:T(8,128)(2,1)S(1)}, bf16[768,1280]{0,1:T(8,128)(2,1)}, u32[]{:S(2)}, u32[]{:S(2)}) %collective-permute-start.2) | collective-permute-done | bytes 1966112 | tf_op jit(solution)/shard_map/ppermute | solution.py:21
  384.3 3.3 collective-permute-start.3
  387.7 42.1 %collective-permute-done.3 = bf16[768,1280]{0,1:T(8,128)(2,1)S(1)} collective-permute-done((bf16[768,1280]{0,1:T(8,128)(2,1)}, bf16[768,1280]{0,1:T(8,128)(2,1)S(1)}, u32[]{:S(2)}, u32[]{:S(2)}) %collective-permute-start.3) | collective-permute-done | bytes 1966112 | tf_op jit(solution)/shard_map/ppermute | solution.py:21
  429.9 0.2 copy.25
  430.1 2.2 fusion.63
  432.3 39.7 %psum.14 = f32[768,16]{0,1:T(8,128)S(1)} all-reduce(f32[768,16]{0,1:T(8,128)S(1)} %fusion.63), channel_id=1, replica_groups=mesh['pipe'=16,'fsdp'=8] {'fsdp'}, use_global_device_ids=true, to_apply=%region_0.0 | all-reduce | flops 12288 | bytes 98304 | tf_op jit(solution)/shard_map/psum | solution.py:99
  472.1 3.1 fusion.81
  475.2 21.7 %fusion.56 = bf16[96,8,8,128]{3,1,2,0:T(8,128)(2,1)} fusion(f32[768,1024]{1,0:T(8,128)} %fusion.81, bf16[768,8192]{1,0:T(8,128)(2,1)} %collective-permute-done.4, bf16[1,1024,8192]{2,1,0:T(8,128)(2,1)} %param.11), kind=kOutput, calls=%fused_computation.56 | convolution fusion | flops 12887261184 | bytes 34078720 | tf_op jit(solution)/shard_map/td,qd->tq/dot_general | solution.py:100
  496.8 3.2 copy.40
  500.0 48.6 %while.17 = (s32[]{:T(128)}, f32[768,1,128]{0,2,1:T(8,128)S(1)}, f32[768,1,128]{0,2,1:T(8,128)S(1)}, bf16[3,256,1,8,128]{4,3,1,0,2:T(8,128)(2,1)}, bf16[3,256,1,...) while((s32[]{:T(128)}, f32[768,1,128]{0,2,1:T(8,128)S(1)}, ...), condition=%wide.region_5.6_spmd.clone, body=%wide.region_1.5_spmd.clone.sunk | while | flops 2456578304 | bytes 51878136 | solution.py:133
  500.0 0.6 dynamic_slice.48
  501.4 0.2 fusion.120
  501.6 1.1 constant_dynamic-slice_fusion.2
  502.7 1.4 fusion.121
  504.1 1.6 fusion.122
  505.7 2.0 fusion.126
  507.7 2.1 fusion.123
  509.8 0.4 multiply_reduce_fusion.2
  510.1 2.8 fusion.124
  512.9 0.7 fusion.125
  513.6 1.0 fusion.127
  514.5 1.7 copy_dynamic-update-slice_fusion.3
  516.2 0.6 dynamic_slice.48
  517.6 0.2 fusion.120
  517.8 1.1 constant_dynamic-slice_fusion.2
  518.9 1.4 fusion.121
  520.3 1.6 fusion.122
  521.8 2.0 fusion.126
  523.9 2.1 fusion.123
  526.0 0.4 multiply_reduce_fusion.2
  526.3 2.8 fusion.124
  529.1 0.7 fusion.125
  529.8 1.0 fusion.127
  530.8 1.7 copy_dynamic-update-slice_fusion.3
  532.4 0.6 dynamic_slice.48
  533.8 0.2 fusion.120
  534.0 1.1 constant_dynamic-slice_fusion.2
  535.1 1.4 fusion.121
  536.4 1.6 fusion.122
  538.0 2.0 fusion.126
  540.1 2.1 fusion.123
  542.2 0.4 multiply_reduce_fusion.2
  542.5 2.8 fusion.124
  545.3 0.7 fusion.125
  546.0 1.0 fusion.127
  547.0 1.7 copy_dynamic-update-slice_fusion.3
  548.6 2.9 fusion.77
  551.5 1.9 fusion.65
  553.5 2.1 broadcast_in_dim_reshape.3
  555.5 38.7 %psum.15 = bf16[768,16]{1,0:T(8,128)(2,1)S(1)} all-reduce(bf16[768,16]{1,0:T(8,128)(2,1)S(1)} %fusion.65), channel_id=1, replica_groups=mesh['pipe'=16,'fsdp'=8] {'fsdp'}, use_global_device_ids=true, to_apply=%region_6.7 | all-reduce | flops 12288 | bytes 49152 | tf_op jit(solution)/shard_map/psum | solution.py:143
  594.2 0.8 copy.29
  595.0 0.8 copy.30
  595.8 2.4 fusion.71
  (38 shorter events, 0.7 us)
Async XLA Ops:
  7.2 464.9 %copy-start = (bf16[1,16,1024]{2,1,0:T(8,128)(2,1)S(1)}, bf16[1,16,1024]{2,1,0:T(8,128)(2,1)}, u32[]{:S(2)}) copy-start(bf16[1,16,1024]{2,1,0:T(8,128)(2,1)} %param.12) | copy-start | bytes 98308
  7.2 157.8 %copy-start.2 = (bf16[1,768,1024]{2,1,0:T(8,128)(2,1)S(1)}, bf16[1,768,1024]{2,1,0:T(8,128)(2,1)}, u32[]{:S(2)}) copy-start(bf16[1,768,1024]{2,1,0:T(8,128)(2,1)} %param.14) | copy-start | bytes 4718596
  7.2 153.1 %all-gather.3.cloned.1.call-start = ((), (), s32[]{:S(2)}) async-start(), calls=%async_computation | async-start | bytes 14155776 | tf_op jit(solution)/shard_map/all_gather | solution.py:89
  160.3 269.8 %collective-permute-start.4 = (bf16[768,8192]{1,0:T(8,128)(2,1)}, bf16[768,8192]{1,0:T(8,128)(2,1)}, u32[]{:S(2)}, u32[]{:S(2)}) collective-permute-start(bf16[768,8192]{1,0:T(8,128)(2,1)} %bitcast.247), channel_id=1, source_target_pairs={{8,0},{16,8},{24,16},{32,24},{40,32},{48,40},{56,48},{64,56},{72,6... | collective-permute-start | bytes 37748744 | tf_op jit(solution)/shard_map/ppermute | solution.py:27
  165.0 222.7 %copy-start.6 = (s32[1,768]{1,0:T(1,128)S(1)}, s32[1,768]{1,0:T(1,128)}, u32[]{:S(2)}) copy-start(s32[1,768]{1,0:T(1,128)} %param.17) | copy-start | bytes 9220
  166.7 263.4 %copy-start.7 = (bf16[1,16,1024]{2,1,0:T(8,128)(2,1)S(1)}, bf16[1,16,1024]{2,1,0:T(8,128)(2,1)}, u32[]{:S(2)}) copy-start(bf16[1,16,1024]{2,1,0:T(8,128)(2,1)} %param.13) | copy-start | bytes 98308
  166.7 15.5 %collective-permute-start = (bf16[768,1280]{0,1:T(8,128)(2,1)S(1)}, bf16[768,1280]{0,1:T(8,128)(2,1)S(1)}, u32[]{:S(2)}, u32[]{:S(2)}) collective-permute-start(bf16[768,1280]{0,1:T(8,128)(2,1)S(1)} %pad_maximum_fusion), channel_id=1, source_target_pairs={{0,8},{8,0},{16,24},{24,16},{32,40},{40,32},{48,56},{56,48},{64,72... | collective-permute-start | bytes 5898248 | tf_op jit(solution)/shard_map/ppermute | solution.py:21
  182.3 157.8 %collective-permute-start.1 = (bf16[768,1280]{0,1:T(8,128)(2,1)S(1)}, bf16[768,1280]{0,1:T(8,128)(2,1)S(1)}, u32[]{:S(2)}, u32[]{:S(2)}) collective-permute-start(bf16[768,1280]{0,1:T(8,128)(2,1)S(1)} %collective-permute-done), channel_id=1, source_target_pairs={{0,16},{16,0},{8,24},{24,8},{32,48},{48,32},{40,56},{56,40},{64,80... | collective-permute-start | bytes 5898248 | tf_op jit(solution)/shard_map/ppermute | solution.py:21
  340.1 44.3 %collective-permute-start.2 = (bf16[768,1280]{0,1:T(8,128)(2,1)S(1)}, bf16[768,1280]{0,1:T(8,128)(2,1)}, u32[]{:S(2)}, u32[]{:S(2)}) collective-permute-start(bf16[768,1280]{0,1:T(8,128)(2,1)S(1)} %collective-permute-done.1), channel_id=1, source_target_pairs={{0,32},{32,0},{8,40},{40,8},{16,48},{48,16},{24,56},{56,24},{64,96... | collective-permute-start | bytes 5898248 | tf_op jit(solution)/shard_map/ppermute | solution.py:21
  384.3 45.4 %collective-permute-start.3 = (bf16[768,1280]{0,1:T(8,128)(2,1)}, bf16[768,1280]{0,1:T(8,128)(2,1)S(1)}, u32[]{:S(2)}, u32[]{:S(2)}) collective-permute-start(bf16[768,1280]{0,1:T(8,128)(2,1)} %collective-permute-done.2), channel_id=1, source_target_pairs={{0,64},{64,0},{8,72},{72,8},{16,80},{80,16},{24,88},{88,24},{32,96... | collective-permute-start | bytes 5898248 | tf_op jit(solution)/shard_map/ppermute | solution.py:21
  429.7 2.6 copy-start.1
  472.0 24.8 %copy-start.4 = (f32[768,16]{0,1:T(8,128)}, f32[768,16]{0,1:T(8,128)S(1)}, u32[]{:S(2)}) copy-start(f32[768,16]{0,1:T(8,128)S(1)} %psum.14) | copy-start | bytes 147460
  496.8 3.2 slice-start
  500.0 48.6 %copy-start.5 = (f32[768,16]{0,1:T(8,128)S(1)}, f32[768,16]{0,1:T(8,128)}, u32[]{:S(2)}) copy-start(f32[768,16]{0,1:T(8,128)} %copy-done.4) | copy-start | bytes 147460
  548.6 4.8 copy-start.3
Sparse Core Ops, SparseCore 0:
  10.3 149.8 all-gather.2
where the time goes:
time: 606 us; the launch traced here: 605 us
  waiting for transfers between devices  410 us (68%)
  blocking collectives  78.4 us (13%)
  matrix products  63.8 us (11%)
  local copies, waits for them, and re-layouts  21 us (3%)
  between operations  14.2 us (2%)
  other arithmetic  7.65 us (1%)
  starting transfers between devices  7.47 us (1%)
    ppermute x4, waiting for transfers between devices, swapped(): return lax.ppermute(block, axis, route)  257 us
    all_gather x1, waiting for transfers between devices, per_device(): lax.all_gather(handoff_gradient[0], 'fsdp', axis=0, tiled=True)  152 us
    psum x1, blocking collectives, per_device(): rank_gradient = lax.psum(rank_portion, 'fsdp')  39.7 us
    psum x1, blocking collectives, per_device(): lax.psum(context_portion.astype(jnp.bfloat16), 'fsdp').astype(jnp.float32)  38.7 us
    dot_general x1, matrix products, per_device(): jnp.einsum('td,qd->tq', incoming_gradient, output_weight[0], preferred_el...  21.7 us
  transfers between devices with their start and end apart: 6, of which 5 were waited for; matrix products, arithmetic and copies ran while one was open for 1% of the time, Pallas kernels for 0%

commit v1 on v0

v1 whole, which is shorter than its diff:
```python
import functools
import math

import jax
import jax.numpy as jnp
from jax import lax
from jax.experimental import pallas as pl
from jax.experimental.pallas import tpu as pltpu
from jax.sharding import PartitionSpec as P

HEAD = 128
KEYS = 512
LORA_SCALE = 2.0
NEG = -1e30
LOG2E = math.log2(math.e)
F32 = jnp.float32
BF16 = jnp.bfloat16
HIGHEST = lax.Precision.HIGHEST
VMEM_BYTES = 44 << 20

NT = (((1,), (1,)), ((), ()))
TN = (((0,), (0,)), ((), ()))
NN = (((1,), (0,)), ((), ()))


def dot(a, b, dims, precision=None):
    return lax.dot_general(a, b, dims, precision=precision, preferred_element_type=F32)


def stack_heads(rows):
    heads = rows.shape[1] // HEAD
    return jnp.concatenate([rows[:, h * HEAD : (h + 1) * HEAD] for h in range(heads)], axis=0)


def unstack_heads(stacked, count):
    heads = stacked.shape[0] // count
    return jnp.concatenate([stacked[h * count : (h + 1) * count] for h in range(heads)], axis=1)


def window_start(block, rows):
    return pl.multiple_of(jnp.maximum(block * rows + rows - KEYS, 0), 32)


def allowed_keys(start, bounds):
    lanes = bounds.shape[1]
    position = start + lax.broadcasted_iota(jnp.int32, (KEYS, lanes), 0)
    return (position >= bounds[0:1]) & (position <= bounds[1:2])


def forward_kernel(rows, q_ref, k_ref, v_ref, bounds_ref, ctx_ref, lse_ref):
    start = window_start(pl.program_id(0), rows)
    keys = k_ref[pl.ds(start, KEYS), :]
    values = v_ref[pl.ds(start, KEYS), :]
    queries = stack_heads(q_ref[...])
    scores = dot(keys, queries, NT) * (LOG2E / math.sqrt(HEAD))
    scores = jnp.where(allowed_keys(start, bounds_ref[0]), scores, NEG)
    top = jnp.max(scores, axis=0, keepdims=True)
    expanded = jnp.exp2(scores - top)
    total = jnp.sum(expanded, axis=0, keepdims=True)
    probs = (expanded / total).astype(BF16)
    context = dot(values, probs, TN)
    ctx_ref[...] = unstack_heads(context.T.astype(BF16), rows)
    lse_ref[0] = top + jnp.log2(total)


def attention_forward(query, key, value, bounds):
    tokens, width = query.shape
    blocks, _, lanes = bounds.shape
    rows = tokens // blocks
    whole = pl.BlockSpec((tokens, HEAD), lambda i: (0, 0))
    return pl.pallas_call(
        functools.partial(forward_kernel, rows),
        grid=(blocks,),
        in_specs=[
            pl.BlockSpec((rows, width), lambda i: (i, 0)),
            whole,
            whole,
            pl.BlockSpec((1, 2, lanes), lambda i: (i, 0, 0)),
        ],
        out_specs=[
            pl.BlockSpec((rows, width), lambda i: (i, 0)),
            pl.BlockSpec((1, 1, lanes), lambda i: (i, 0, 0)),
        ],
        out_shape=[
            jax.ShapeDtypeStruct((tokens, width), BF16),
            jax.ShapeDtypeStruct((blocks, 1, lanes), F32),
        ],
        compiler_params=pltpu.CompilerParams(vmem_limit_bytes=VMEM_BYTES),
        cost_estimate=pl.CostEstimate(
            flops=4 * tokens * KEYS * width,
            bytes_accessed=4 * tokens * width,
            transcendentals=blocks * KEYS * lanes,
        ),
        name="attention_forward",
    )(query, key, value, bounds)


def project_kernel(parts, w_ref, up_ref, down_ref, *refs):
    x_refs = refs[:parts]
    g_ref, rank_ref, acc, rank_acc = refs[parts:]
    step = pl.program_id(0)
    x = jnp.concatenate([r[...] for r in x_refs], axis=0)
    product = dot(x, w_ref[...], NT)
    rank = dot(x, up_ref[...], NT)

    @pl.when(step == 0)
    def _():
        acc[...] = product
        rank_acc[...] = rank

    @pl.when(step > 0)
    def _():
        acc[...] += product
        rank_acc[...] += rank

    @pl.when(step == pl.num_programs(0) - 1)
    def _():
        projected = dot(rank_acc[...], down_ref[...].astype(F32), NN, HIGHEST)
        g_ref[...] = (acc[...] + LORA_SCALE * projected).astype(BF16)
        rank_ref[...] = rank_acc[...]


def project(xs, weight, up, down):
    features, depth = weight.shape
    ranks = up.shape[0]
    rows = sum(x.shape[0] for x in xs)
    chunk = 1024
    return pl.pallas_call(
        functools.partial(project_kernel, len(xs)),
        grid=(depth // chunk,),
        in_specs=[
            pl.BlockSpec((features, chunk), lambda i: (0, i)),
            pl.BlockSpec((ranks, chunk), lambda i: (0, i)),
            pl.BlockSpec((ranks, features), lambda i: (0, 0)),
        ]
        + [pl.BlockSpec((x.shape[0], chunk), lambda i: (0, i)) for x in xs],
        out_specs=[
            pl.BlockSpec((rows, features), lambda i: (0, 0)),
            pl.BlockSpec((rows, ranks), lambda i: (0, 0)),
        ],
        out_shape=[
            jax.ShapeDtypeStruct((rows, features), BF16),
            jax.ShapeDtypeStruct((rows, ranks), F32),
        ],
        scratch_shapes=[pltpu.VMEM((rows, features), F32), pltpu.VMEM((rows, ranks), F32)],
        compiler_params=pltpu.CompilerParams(vmem_limit_bytes=VMEM_BYTES),
        cost_estimate=pl.CostEstimate(
            flops=2 * rows * features * depth,
            bytes_accessed=2 * features * depth + 2 * rows * depth,
            transcendentals=0,
        ),
        name="project",
    )(weight, up, down, *xs)


def backward_kernel(first, last, rows, where_ref, *refs):
    q_ref, ctx_ref, lse_ref, bounds_ref, g_ref, rank_ref, k_ref, v_ref = refs[:8]
    refs = refs[8:]
    if not first:
        dq_in, dk_in, dv_in, dm_in = refs[:4]
        refs = refs[4:]
    dq_ref, dk_ref, dv_ref, dm_ref, dk, dv, dm = refs
    step = pl.program_id(0)

    @pl.when(step == 0)
    def _():
        if first:
            dk[...] = jnp.zeros_like(dk)
            dv[...] = jnp.zeros_like(dv)
            dm[...] = jnp.zeros_like(dm)
        else:
            dk[...] = dk_in[...]
            dv[...] = dv_in[...]
            dm[...] = dm_in[...]

    start = window_start(where_ref[step], rows)
    window = pl.ds(start, KEYS)
    keys = k_ref[window, :]
    values = v_ref[window, :]
    queries = stack_heads(q_ref[...])
    gradient = stack_heads(g_ref[...])
    context = stack_heads(ctx_ref[...])
    products = gradient.astype(F32) * context.astype(F32)
    delta = dot(jnp.ones((8, HEAD), F32), products, NT, HIGHEST)[0:1]
    scores = dot(keys, queries, NT) * (LOG2E / math.sqrt(HEAD))
    shifted = jnp.where(allowed_keys(start, bounds_ref[0]), scores - lse_ref[0], NEG)
    probs = jnp.exp2(shifted)
    grad_probs = dot(values, gradient, NT)
    grad_scores = (probs * (grad_probs - delta)).astype(BF16)
    dv[window, :] += dot(probs.astype(BF16), gradient, NN)
    dk[window, :] += dot(grad_scores, queries, NN)
    grad_query = dot(keys, grad_scores, TN) * (1.0 / math.sqrt(HEAD))
    dq_ref[...] = unstack_heads(grad_query.T.astype(BF16), rows)
    dm[...] += dot(rank_ref[...], ctx_ref[...].astype(F32), TN, HIGHEST)

    @pl.when(step == pl.num_programs(0) - 1)
    def _():
        if last:
            tokens = k_ref.shape[0]
            dk_ref[...] = (dk[...] * (1.0 / math.sqrt(HEAD))).astype(BF16)
            dv_ref[...] = dv[...].astype(BF16)
            dm_ref[...] = dm[...] * (LORA_SCALE / math.sqrt(tokens))
        else:
            dk_ref[...] = dk[...]
            dv_ref[...] = dv[...]
            dm_ref[...] = dm[...]


def attention_backward(where, query, context, lse, bounds, gradient, rank, key, value, carried, last):
    tokens, width = query.shape
    blocks, _, lanes = bounds.shape
    rows = tokens // blocks
    ranks = rank.shape[1]
    steps = gradient.shape[0] // rows
    first = carried is None
    whole = pl.BlockSpec((tokens, HEAD), lambda i, w: (0, 0))
    small = pl.BlockSpec((ranks, width), lambda i, w: (0, 0))
    picked = pl.BlockSpec((rows, width), lambda i, w: (w[i], 0))
    in_specs = [
        picked,
        picked,
        pl.BlockSpec((1, 1, lanes), lambda i, w: (w[i], 0, 0)),
        pl.BlockSpec((1, 2, lanes), lambda i, w: (w[i], 0, 0)),
        pl.BlockSpec((rows, width), lambda i, w: (i, 0)),
        pl.BlockSpec((rows, ranks), lambda i, w: (i, 0)),
        whole,
        whole,
    ]
    operands = [query, context, lse, bounds, gradient, rank, key, value]
    aliases = {}
    if not first:
        in_specs += [pl.BlockSpec(memory_space=pl.ANY), whole, whole, small]
        operands += list(carried)
        aliases = {9: 0}
    kv_type = BF16 if last else F32
    return pl.pallas_call(
        functools.partial(backward_kernel, first, last, rows),
        grid_spec=pltpu.PrefetchScalarGridSpec(
            num_scalar_prefetch=1,
            grid=(steps,),
            in_specs=in_specs,
            out_specs=[picked, whole, whole, small],
            scratch_shapes=[
                pltpu.VMEM((tokens, HEAD), F32),
                pltpu.VMEM((tokens, HEAD), F32),
                pltpu.VMEM((ranks, width), F32),
            ],
        ),
        out_shape=[
            jax.ShapeDtypeStruct((tokens, width), BF16),
            jax.ShapeDtypeStruct((tokens, HEAD), kv_type),
            jax.ShapeDtypeStruct((tokens, HEAD), kv_type),
            jax.ShapeDtypeStruct((ranks, width), F32),
        ],
        input_output_aliases=aliases,
        compiler_params=pltpu.CompilerParams(vmem_limit_bytes=VMEM_BYTES),
        cost_estimate=pl.CostEstimate(
            flops=10 * steps * rows * KEYS * width,
            bytes_accessed=10 * steps * rows * width,
            transcendentals=steps * KEYS * lanes,
        ),
        name="attention_backward",
    )(where, *operands)


def up_map_kernel(where_ref, member_ref, *refs):
    rank_ref, x_ref, out_ref = refs[0], refs[1:-1], refs[-1]
    rows = rank_ref.shape[0] // 8
    total = None
    offset = 0
    for ref in x_ref:
        count = ref.shape[0]
        block, inner = offset // rows, offset % rows
        begin = pl.multiple_of(where_ref[block] * rows + inner, 16)
        part = dot(rank_ref[pl.ds(begin, count), :], ref[...].astype(F32), TN, HIGHEST)
        total = part if total is None else total + part
        offset += count
    out_ref[...] = total * (LORA_SCALE / math.sqrt(rank_ref.shape[0]))


def up_map(where, member, rank_context, xs, width):
    tokens, ranks = rank_context.shape
    return pl.pallas_call(
        up_map_kernel,
        grid_spec=pltpu.PrefetchScalarGridSpec(
            num_scalar_prefetch=2,
            grid=(1,),
            in_specs=[pl.BlockSpec((tokens, ranks), lambda i, w, m: (0, 0))]
            + [pl.BlockSpec((x.shape[0], width), lambda i, w, m: (0, m[0])) for x in xs],
            out_specs=pl.BlockSpec((ranks, width), lambda i, w, m: (0, 0)),
        ),
        out_shape=jax.ShapeDtypeStruct((ranks, width), F32),
        compiler_params=pltpu.CompilerParams(vmem_limit_bytes=VMEM_BYTES),
        name="up_map",
    )(where, member, rank_context, *xs)


def per_device(
    handoff_gradient,
    output_weight,
    adapter_down,
    adapter_up,
    stored_queries,
    stored_keys,
    stored_values,
    segments,
):
    stages = lax.axis_size("pipe")
    members = lax.axis_size("fsdp")
    ring = members // 2
    both = ("pipe", "fsdp")
    member = lax.axis_index("fsdp")
    shard = handoff_gradient[0]
    rows = shard.shape[0]
    half = rows // 2
    tokens = rows * members
    heads = stored_queries.shape[2] // HEAD

    def from_next(block, flip):
        route = []
        for p in range(stages):
            for f in range(members):
                source = ((p + 1) % stages) * members + (f + flip) % members
                route.append((source, p * members + f))
        return lax.ppermute(block, both, route)

    def along_x(block, distance):
        route = []
        for f in range(members):
            plane, x = divmod(f, ring)
            route.append((plane * ring + (x - distance) % ring, f))
        return lax.ppermute(block, "fsdp", route)

    def mirrored(block):
        return lax.ppermute(block, "pipe", [(i, stages - 1 - i) for i in range(stages)])

    near = from_next(shard, 0)
    across = from_next(shard, ring)
    query = mirrored(stored_queries[0])
    key = mirrored(stored_keys[0])
    value = mirrored(stored_values[0])
    up_whole = lax.all_gather(adapter_up[0], "fsdp", axis=1, tiled=True)
    down = adapter_down[0]

    left0 = along_x(near, 1)
    right0 = along_x(near, -1)
    left1 = along_x(across, 1)
    right1 = along_x(across, -1)
    far0 = (along_x(left0[:half], 1), along_x(right0[half:], -1))
    far1 = (along_x(left1[:half], 1), along_x(right1[half:], -1))

    plane, x = member // ring, member % ring

    def pair(shift):
        column = (x + shift) % ring
        return jnp.stack([plane * ring + column, (1 - plane) * ring + column]).astype(jnp.int32)

    doc = segments[0]
    position = jnp.arange(tokens, dtype=jnp.int32)
    begin = jnp.sum((doc[None, :] < doc[:, None]).astype(jnp.int32), axis=1)
    bounds = jnp.stack([begin, position]).reshape(2, members, rows)
    bounds = jnp.tile(bounds.transpose(1, 0, 2), (1, 1, heads))

    weight = output_weight[0]
    context, lse = attention_forward(query, key, value, bounds)
    rank_context = lax.dot_general(down, context, NT, preferred_element_type=F32)
    for partner in (1, 2, ring):
        route = [(f, f ^ partner) for f in range(members)]
        rank_context = rank_context + lax.ppermute(rank_context, "fsdp", route)

    groups = [
        (pair(0), [near, across]),
        (pair(-1), [left0, left1]),
        (pair(1), [right0, right1]),
        (pair(2), [far0[0], far0[1], far1[0], far1[1]]),
    ]
    carried = None
    for number, (where, xs) in enumerate(groups):
        gradient, rank = project(xs, weight, up_whole, down)
        carried = attention_backward(
            where,
            query,
            context,
            lse,
            bounds,
            gradient,
            rank,
            key,
            value,
            carried,
            number == len(groups) - 1,
        )
    query_gradient, key_gradient, value_gradient, down_map_gradient = carried
    up_map_gradient = up_map(
        jnp.concatenate([where for where, _ in groups]),
        member.reshape(1).astype(jnp.int32),
        rank_context.T,
        [x for _, xs in groups for x in xs],
        adapter_up.shape[2],
    )
    return (
        query_gradient[None],
        key_gradient[None],
        value_gradient[None],
        down_map_gradient[None],
        up_map_gradient[None],
    )


def solution(mesh):
    split = P("pipe", None, "fsdp")
    rows = P("pipe", "fsdp", None)
    return jax.shard_map(
        per_device,
        mesh=mesh,
        in_specs=(rows, rows, split, split, split, split, split, P("pipe", None)),
        out_specs=(split,) * 5,
        check_vma=False,
    )
```

time: 606 us -> 299 us (0.49)
  waiting for transfers between devices: 410 us -> 78.7 us
  Pallas kernels: 0 us -> 82.8 us
  matrix products: 63.8 us -> 1.29 us
  starting transfers between devices: 7.47 us -> 32.9 us
  local copies, waits for them, and re-layouts: 21 us -> 6.9 us
  between operations: 14.2 us -> 0.8 us
  blocking collectives: 78.4 us -> 91.3 us
    ppermute x5 -> x16, waiting for transfers between devices: 257 us -> 78.7 us  [the longest x2 68.6 us: from_next(): return lax.ppermute(block, both, route)]
    all_gather x1 -> x0, waiting for transfers between devices: 152 us -> none  [per_device(): lax.all_gather(handoff_gradient[0], 'fsdp', axis=0, tiled=True)]
    all_gather x0 -> x1, blocking collectives: none -> 91.3 us  [per_device(): up_whole = lax.all_gather(adapter_up[0], 'fsdp', axis=1, tiled=True)]
    pallas_call x0 -> x10, Pallas kernels: none -> 82.8 us  [the longest x4 51.1 us: project(): pl.pallas_call(functools.partial(project_kernel, len(xs)), grid=(depth //...]
    psum x2 -> x0, blocking collectives: 78.4 us -> none  [the longest x1 39.7 us: per_device(): rank_gradient = lax.psum(rank_portion, 'fsdp')]
    dot_general x24 -> x1, matrix products: 63.8 us -> 1.29 us  [per_device(): lax.dot_general(down, context, NT, preferred_element_type=F32)]
    ppermute x5 -> x16, starting transfers between devices: 7.43 us -> 32.9 us  [the longest x8 13.4 us: along_x(): return lax.ppermute(block, 'fsdp', route)]
  transfers between devices with their start and end apart: 6 -> 16, of which waited for: 5 -> 3; matrix products, arithmetic and copies ran while one was open for 1% -> 3% of each run, Pallas kernels for 0% -> 21%
where the time goes in v1:
time: 299 us; the launch traced here: 297 us
  blocking collectives  91.3 us (31%)
  Pallas kernels  82.8 us (28%)
  waiting for transfers between devices  78.7 us (26%)
  starting transfers between devices  32.9 us (11%)
  local copies, waits for them, and re-layouts  6.9 us (2%)
    all_gather x1, blocking collectives, per_device(): up_whole = lax.all_gather(adapter_up[0], 'fsdp', axis=1, tiled=True)  91.3 us
    ppermute x2, waiting for transfers between devices, from_next(): return lax.ppermute(block, both, route)  68.6 us
    pallas_call x4, Pallas kernels, project(): pl.pallas_call(functools.partial(project_kernel, len(xs)), grid=(depth //...  51.1 us
    pallas_call x4, Pallas kernels, attention_backward(): pl.pallas_call(functools.partial(backward_kernel, first, last, rows), gri...  19.1 us
    ppermute x8, starting transfers between devices, along_x(): return lax.ppermute(block, 'fsdp', route)  13.4 us
    ppermute x3, waiting for transfers between devices, per_device(): rank_context = rank_context + lax.ppermute(rank_context, 'fsdp', route)  10.1 us
    pallas_call x1, Pallas kernels, attention_forward(): pl.pallas_call(functools.partial(forward_kernel, rows), grid=(blocks,), i...  8.63 us
    ppermute x3, starting transfers between devices, per_device(): rank_context = rank_context + lax.ppermute(rank_context, 'fsdp', route)  8.41 us
  transfers between devices with their start and end apart: 16, of which 3 were waited for; matrix products, arithmetic and copies ran while one was open for 3% of the time, Pallas kernels for 21%

profile of v1, /device:TPU:0, one launch (start us, length us, event | category | flops | bytes accessed | tf_op | source)
XLA Modules:
  0.0 297.4 jit_solution(16510243535278262142)
XLA Ops:
  0.6 6.1 %collective-permute-start.8 = (bf16[96,8192]{1,0:T(8,128)(2,1)}, bf16[96,8192]{1,0:T(8,128)(2,1)}, u32[]{:S(2)}, u32[]{:S(2)}) collective-permute-start(bf16[96,8192]{1,0:T(8,128)(2,1)} %bitcast.46), channel_id=1, source_target_pairs={{12,0},{13,1},{14,2},{15,3},{8,4},{9,5},{10,6},{11,7},{20,8},{21,9... | collective-permute-start | bytes 4718600 | tf_op jit(solution)/shard_map/ppermute | solution.py:325
  6.7 1.1 collective-permute-start.3
  7.8 0.0 collective-permute-start
  7.9 3.8 %collective-permute-start.1 = (bf16[768,128]{1,0:T(8,128)(2,1)}, bf16[768,128]{1,0:T(8,128)(2,1)S(1)}, u32[]{:S(2)}, u32[]{:S(2)}) collective-permute-start(bf16[768,128]{1,0:T(8,128)(2,1)} %bitcast.49), channel_id=1, source_target_pairs={{0,120},{8,112},{16,104},{24,96},{32,88},{40,80},{48,72},{56,64},{... | collective-permute-start | bytes 589832 | tf_op jit(solution)/shard_map/ppermute | solution.py:335
  11.7 0.0 collective-permute-start.2
  11.8 0.7 reduce
  12.5 0.4 convert_reduce_fusion
  12.8 0.1 stack.52
  12.9 68.6 %collective-permute-done.8.refs_1_.refs_2_ = bf16[96,8192]{1,0:T(8,128)(2,1)} collective-permute-done((bf16[96,8192]{1,0:T(8,128)(2,1)}, bf16[96,8192]{1,0:T(8,128)(2,1)}, u32[]{:S(2)}, u32[]{:S(2)}) %collective-permute-start.8) | collective-permute-done | bytes 1572896 | tf_op jit(solution)/shard_map/ppermute | solution.py:325
  81.5 1.5 collective-permute-start.9
  83.0 0.0 collective-permute-done.1.k_ref.refs_6_
  83.0 1.7 collective-permute-start.11
  84.8 0.0 collective-permute-done.3.refs_0_.refs_1_
  84.8 0.3 collective-permute-start.4
  85.1 0.0 collective-permute-done.2.v_ref.refs_7_
  85.1 3.0 collective-permute-start.6
  88.0 0.1 pad_add_fusion.3.where_ref
  88.1 0.1 tile.10.bounds_ref.refs_3_
  88.2 0.1 pad_add_fusion.2.where_ref
  88.3 0.1 pad_add_fusion.1.where_ref
  88.4 91.3 %all-gather = bf16[1,16,8192]{2,1,0:T(8,128)(2,1)S(1)} all-gather(bf16[1,16,1024]{2,1,0:T(8,128)(2,1)} %param.11), channel_id=2, replica_groups=mesh['pipe'=16,'fsdp'=8] {'fsdp'}, dimensions={2}, use_global_device_ids=true | all-gather | bytes 294912 | tf_op jit(solution)/shard_map/all_gather | solution.py:342
  179.7 0.0 copy-done
  179.7 0.0 copy-done.3
  179.7 0.0 collective-permute-done.q_ref.refs_0_
  179.8 0.0 copy-start.1
  179.8 0.9 copy-done.1
  180.7 0.9 copy-done.4
  181.6 8.6 %attention_forward.1 = (bf16[768,1024]{1,0:T(8,128)(2,1)S(1)}, f32[8,1,768]{2,1,0:T(1,128)S(1)}) custom-call(bf16[768,1024]{1,0:T(8,128)(2,1)S(1)} %collective-permute-done.q_ref.refs_0_, bf16[768,128]{1,0:T(8,128)(2,1)S(1)} %copy-done.1, bf16[768,128]{1,0:T(8,128)(2,1)S(1)} %copy-done.4, s32[8,2,768]{2,1,0:T(2,128)S(1)} %tile.10.bounds_ref.refs_3_), custom_call_target="tpu_custom_call" | custom-call | flops 1610612736 | bytes 3145728 | tf_op jit(solution)/shard_map/attention_forward/pallas_call | solution.py:71
  190.3 1.3 convolution_bitcast_fusion
  191.6 1.9 collective-permute-start.13
  193.4 0.1 pad_add_fusion.where_ref
  193.5 0.1 concatenate.5.where_ref
  193.6 9.1 %collective-permute-done.13 = f32[16,768]{0,1:T(8,128)} collective-permute-done((f32[16,768]{0,1:T(8,128)}, f32[16,768]{0,1:T(8,128)}, u32[]{:S(2)}, u32[]{:S(2)}) %collective-permute-start.13) | collective-permute-done | bytes 49184 | tf_op jit(solution)/shard_map/ppermute | solution.py:369
  202.6 1.2 add.82
  203.8 1.4 collective-permute-start.14
  205.2 12.9 %project.7 = (bf16[192,1024]{1,0:T(8,128)(2,1)S(1)}, f32[192,16]{1,0:T(8,128)S(1)}) custom-call(bf16[1024,8192]{1,0:T(8,128)(2,1)} %bitcast.40, bf16[16,8192]{1,0:T(8,128)(2,1)S(1)} %bitcast.32, bf16[16,1024]{1,0:T(8,128)(2,1)S(1)} %bitcast.36, bf16[96,8192]{1,0:T(8,128)(2,1)} %collective-permute-done.3.refs_0_.refs_1_, ...), custom_call_target="tpu_custom_call" | custom-call | flops 3221225472 | bytes 19922944 | tf_op jit(solution)/shard_map/project/pallas_call | solution.py:128
  218.0 0.0 collective-permute-done.14
  218.1 5.2 %collective-permute-start.15 = (f32[16,768]{0,1:T(8,128)S(1)}, f32[16,768]{0,1:T(8,128)S(1)}, u32[]{:S(2)}, u32[]{:S(2)}) collective-permute-start(f32[16,768]{0,1:T(8,128)S(1)} %add.83), channel_id=1, source_target_pairs={{0,4},{1,5},{2,6},{3,7},{4,0},{5,1},{6,2},{7,3},{8,12},{9,13},{10,... | collective-permute-start | bytes 147464 | tf_op jit(solution)/shard_map/ppermute | solution.py:369
  223.3 0.0 copy-done.5
  223.3 4.7 %attention_backward.4 = (bf16[768,1024]{1,0:T(8,128)(2,1)}, f32[768,128]{1,0:T(8,128)S(1)}, f32[768,128]{1,0:T(8,128)S(1)}, f32[16,1024]{1,0:T(8,128)S(1)}) custom-call(s32[2]{0:T(128)S(1)} %pad_add_fusion.3.where_ref, bf16[768,1024]{1,0:T(8,128)(2,1)S(1)} %collective-permute-done.q_ref.refs_0_, bf16[768,1024]{1,0:T(8,128)(2,1)S(1)} %get-tuple-element.31.refs_1_, ...), custom_call_target="tpu_custom_call" | custom-call | flops 1006632960 | bytes 1966080 | tf_op jit(solution)/shard_map/attention_backward/pallas_call | solution.py:236
  228.0 1.0 collective-permute-done.15
  229.1 0.0 collective-permute-done.9.refs_1_.refs_4_
  229.1 1.2 slice.18
  230.3 1.3 collective-permute-start.10
  231.6 0.0 collective-permute-done.11.refs_1_.refs_6_
  231.6 1.2 slice.19
  232.8 2.1 collective-permute-start.12
  234.9 0.0 collective-permute-done.4.refs_0_.refs_3_
  234.9 1.2 slice.16
  236.0 0.1 collective-permute-start.5
  236.1 0.0 collective-permute-done.6.refs_0_.refs_5_
  236.1 1.2 slice.17
  237.3 3.5 %collective-permute-start.7 = (bf16[48,8192]{1,0:T(8,128)(2,1)S(1)}, bf16[48,8192]{1,0:T(8,128)(2,1)S(1)}, u32[]{:S(2)}, u32[]{:S(2)}) collective-permute-start(bf16[48,8192]{1,0:T(8,128)(2,1)S(1)} %slice.17), channel_id=1, source_target_pairs={{1,0},{2,1},{3,2},{0,3},{5,4},{6,5},{7,6},{4,7},{9,8},{10,9},{11,1... | collective-permute-start | bytes 2359304 | tf_op jit(solution)/shard_map/ppermute | solution.py:332
  240.8 12.8 %project.6 = (bf16[192,1024]{1,0:T(8,128)(2,1)S(1)}, f32[192,16]{1,0:T(8,128)S(1)}) custom-call(bf16[1024,8192]{1,0:T(8,128)(2,1)} %bitcast.41, bf16[16,8192]{1,0:T(8,128)(2,1)S(1)} %bitcast.33, bf16[16,1024]{1,0:T(8,128)(2,1)S(1)} %bitcast.37, bf16[96,8192]{1,0:T(8,128)(2,1)} %collective-permute-done.4.refs_0_.refs_3_, ...), custom_call_target="tpu_custom_call" | custom-call | flops 3221225472 | bytes 19922944 | tf_op jit(solution)/shard_map/project/pallas_call | solution.py:128
  253.6 4.7 %attention_backward.5 = (bf16[768,1024]{1,0:T(8,128)(2,1)}, f32[768,128]{1,0:T(8,128)S(1)}, f32[768,128]{1,0:T(8,128)S(1)}, f32[16,1024]{1,0:T(8,128)S(1)}) custom-call(s32[2]{0:T(128)S(1)} %pad_add_fusion.2.where_ref, bf16[768,1024]{1,0:T(8,128)(2,1)S(1)} %collective-permute-done.q_ref.refs_0_, ...), custom_call_target="tpu_custom_call", output_to_operand_aliasing={{0}: (9, {})} | custom-call | flops 1006632960 | bytes 1966080 | tf_op jit(solution)/shard_map/attention_backward/pallas_call | solution.py:236
  258.4 12.8 %project.5 = (bf16[192,1024]{1,0:T(8,128)(2,1)S(1)}, f32[192,16]{1,0:T(8,128)S(1)}) custom-call(bf16[1024,8192]{1,0:T(8,128)(2,1)} %bitcast.42, bf16[16,8192]{1,0:T(8,128)(2,1)S(1)} %bitcast.34, bf16[16,1024]{1,0:T(8,128)(2,1)S(1)} %bitcast.38, bf16[96,8192]{1,0:T(8,128)(2,1)} %collective-permute-done.6.refs_0_.refs_5_, ...), custom_call_target="tpu_custom_call" | custom-call | flops 3221225472 | bytes 19922944 | tf_op jit(solution)/shard_map/project/pallas_call | solution.py:128
  271.2 4.8 %attention_backward.6 = (bf16[768,1024]{1,0:T(8,128)(2,1)}, f32[768,128]{1,0:T(8,128)S(1)}, f32[768,128]{1,0:T(8,128)S(1)}, f32[16,1024]{1,0:T(8,128)S(1)}) custom-call(s32[2]{0:T(128)S(1)} %pad_add_fusion.1.where_ref, bf16[768,1024]{1,0:T(8,128)(2,1)S(1)} %collective-permute-done.q_ref.refs_0_, ...), custom_call_target="tpu_custom_call", output_to_operand_aliasing={{0}: (9, {})} | custom-call | flops 1006632960 | bytes 1966080 | tf_op jit(solution)/shard_map/attention_backward/pallas_call | solution.py:236
  275.9 0.0 collective-permute-done.10.refs_2_.refs_9_
  275.9 0.0 collective-permute-done.12.refs_3_.refs_10_
  275.9 0.0 collective-permute-done.5.refs_0_.refs_7_
  275.9 0.0 collective-permute-done.7.refs_1_.refs_8_
  276.0 12.6 %project.4 = (bf16[192,1024]{1,0:T(8,128)(2,1)S(1)}, f32[192,16]{1,0:T(8,128)S(1)}) custom-call(bf16[1024,8192]{1,0:T(8,128)(2,1)} %bitcast.43, bf16[16,8192]{1,0:T(8,128)(2,1)S(1)} %bitcast.35, bf16[16,1024]{1,0:T(8,128)(2,1)S(1)} %bitcast.39, bf16[48,8192]{1,0:T(8,128)(2,1)S(1)} %collective-permute-done.5.refs_0_.refs_7_, ...), custom_call_target="tpu_custom_call" | custom-call | flops 3221225472 | bytes 19922944 | tf_op jit(solution)/shard_map/project/pallas_call | solution.py:128
  288.6 4.0 %up_map.1 = f32[16,1024]{1,0:T(8,128)} custom-call(s32[8]{0:T(128)S(1)} %concatenate.5.where_ref, s32[1]{0:T(128)} %bitcast.20.member_ref, f32[768,16]{1,0:T(8,128)S(1)} %add_bitcast_fusion.refs_0_, bf16[96,8192]{1,0:T(8,128)(2,1)} %collective-permute-done.3.refs_0_.refs_1_, bf16[96,8192]{1,0:T(8,128)(2,1)} %collective-permute-done.8.refs_1_.refs_2_, ...), custom_call_target="tpu_custom_call" | custom-call | tf_op jit(solution)/shard_map/up_map/pallas_call | solution.py:283
  292.5 4.9 %attention_backward.7 = (bf16[768,1024]{1,0:T(8,128)(2,1)}, bf16[768,128]{1,0:T(8,128)(2,1)}, bf16[768,128]{1,0:T(8,128)(2,1)}, f32[16,1024]{1,0:T(8,128)}) custom-call(s32[2]{0:T(128)S(1)} %pad_add_fusion.where_ref, bf16[768,1024]{1,0:T(8,128)(2,1)S(1)} %collective-permute-done.q_ref.refs_0_, ...), custom_call_target="tpu_custom_call", output_to_operand_aliasing={{0}: (9, {})} | custom-call | flops 1006632960 | bytes 1966080 | tf_op jit(solution)/shard_map/attention_backward/pallas_call | solution.py:236
  (13 shorter events, 0.1 us)
Async XLA Ops:
  0.6 80.9 %collective-permute-start.8 = (bf16[96,8192]{1,0:T(8,128)(2,1)}, bf16[96,8192]{1,0:T(8,128)(2,1)}, u32[]{:S(2)}, u32[]{:S(2)}) collective-permute-start(bf16[96,8192]{1,0:T(8,128)(2,1)} %bitcast.46), channel_id=1, source_target_pairs={{12,0},{13,1},{14,2},{15,3},{8,4},{9,5},{10,6},{11,7},{20,8},{21,9... | collective-permute-start | bytes 4718600 | tf_op jit(solution)/shard_map/ppermute | solution.py:325
  6.7 78.1 %collective-permute-start.3 = (bf16[96,8192]{1,0:T(8,128)(2,1)}, bf16[96,8192]{1,0:T(8,128)(2,1)}, u32[]{:S(2)}, u32[]{:S(2)}) collective-permute-start(bf16[96,8192]{1,0:T(8,128)(2,1)} %bitcast.47), channel_id=1, source_target_pairs={{8,0},{9,1},{10,2},{11,3},{12,4},{13,5},{14,6},{15,7},{16,8},{17,9... | collective-permute-start | bytes 4718600 | tf_op jit(solution)/shard_map/ppermute | solution.py:325
  7.8 171.9 %collective-permute-start = (bf16[768,1024]{1,0:T(8,128)(2,1)}, bf16[768,1024]{1,0:T(8,128)(2,1)S(1)}, u32[]{:S(2)}, u32[]{:S(2)}) collective-permute-start(bf16[768,1024]{1,0:T(8,128)(2,1)} %bitcast.48), channel_id=1, source_target_pairs={{0,120},{8,112},{16,104},{24,96},{32,88},{40,80},{48,72},{56,64},{... | collective-permute-start | bytes 4718600 | tf_op jit(solution)/shard_map/ppermute | solution.py:335
  7.9 75.2 %collective-permute-start.1 = (bf16[768,128]{1,0:T(8,128)(2,1)}, bf16[768,128]{1,0:T(8,128)(2,1)S(1)}, u32[]{:S(2)}, u32[]{:S(2)}) collective-permute-start(bf16[768,128]{1,0:T(8,128)(2,1)} %bitcast.49), channel_id=1, source_target_pairs={{0,120},{8,112},{16,104},{24,96},{32,88},{40,80},{48,72},{56,64},{... | collective-permute-start | bytes 589832 | tf_op jit(solution)/shard_map/ppermute | solution.py:335
  11.7 73.4 %collective-permute-start.2 = (bf16[768,128]{1,0:T(8,128)(2,1)}, bf16[768,128]{1,0:T(8,128)(2,1)S(1)}, u32[]{:S(2)}, u32[]{:S(2)}) collective-permute-start(bf16[768,128]{1,0:T(8,128)(2,1)} %bitcast.50), channel_id=1, source_target_pairs={{0,120},{8,112},{16,104},{24,96},{32,88},{40,80},{48,72},{56,64},{... | collective-permute-start | bytes 589832 | tf_op jit(solution)/shard_map/ppermute | solution.py:335
  81.5 147.5 %collective-permute-start.9 = (bf16[96,8192]{1,0:T(8,128)(2,1)}, bf16[96,8192]{1,0:T(8,128)(2,1)}, u32[]{:S(2)}, u32[]{:S(2)}) collective-permute-start(bf16[96,8192]{1,0:T(8,128)(2,1)} %collective-permute-done.8.refs_1_.refs_2_), channel_id=1, source_target_pairs={{3,0},{0,1},{1,2},{2,3},{7,4},{4,5},{5,6},{6,7},{11,8},{8,9},{9,10... | collective-permute-start | bytes 4718600 | tf_op jit(solution)/shard_map/ppermute | solution.py:332
  83.0 96.7 %copy-start = (bf16[768,128]{1,0:T(8,128)(2,1)}, bf16[768,128]{1,0:T(8,128)(2,1)S(1)}, u32[]{:S(2)}) copy-start(bf16[768,128]{1,0:T(8,128)(2,1)S(1)} %collective-permute-done.1.k_ref.refs_6_) | copy-start | bytes 589828
  83.0 148.5 %collective-permute-start.11 = (bf16[96,8192]{1,0:T(8,128)(2,1)}, bf16[96,8192]{1,0:T(8,128)(2,1)}, u32[]{:S(2)}, u32[]{:S(2)}) collective-permute-start(bf16[96,8192]{1,0:T(8,128)(2,1)} %collective-permute-done.8.refs_1_.refs_2_), channel_id=1, source_target_pairs={{1,0},{2,1},{3,2},{0,3},{5,4},{6,5},{7,6},{4,7},{9,8},{10,9},{11,1... | collective-permute-start | bytes 4718600 | tf_op jit(solution)/shard_map/ppermute | solution.py:332
  84.8 150.1 %collective-permute-start.4 = (bf16[96,8192]{1,0:T(8,128)(2,1)}, bf16[96,8192]{1,0:T(8,128)(2,1)}, u32[]{:S(2)}, u32[]{:S(2)}) collective-permute-start(bf16[96,8192]{1,0:T(8,128)(2,1)} %collective-permute-done.3.refs_0_.refs_1_), channel_id=1, source_target_pairs={{3,0},{0,1},{1,2},{2,3},{7,4},{4,5},{5,6},{6,7},{11,8},{8,9},{9,10... | collective-permute-start | bytes 4718600 | tf_op jit(solution)/shard_map/ppermute | solution.py:332
  85.1 94.7 %copy-start.3 = (bf16[768,128]{1,0:T(8,128)(2,1)}, bf16[768,128]{1,0:T(8,128)(2,1)S(1)}, u32[]{:S(2)}) copy-start(bf16[768,128]{1,0:T(8,128)(2,1)S(1)} %collective-permute-done.2.v_ref.refs_7_) | copy-start | bytes 589828
  85.1 151.1 %collective-permute-start.6 = (bf16[96,8192]{1,0:T(8,128)(2,1)}, bf16[96,8192]{1,0:T(8,128)(2,1)}, u32[]{:S(2)}, u32[]{:S(2)}) collective-permute-start(bf16[96,8192]{1,0:T(8,128)(2,1)} %collective-permute-done.3.refs_0_.refs_1_), channel_id=1, source_target_pairs={{1,0},{2,1},{3,2},{0,3},{5,4},{6,5},{7,6},{4,7},{9,8},{10,9},{11,1... | collective-permute-start | bytes 4718600 | tf_op jit(solution)/shard_map/ppermute | solution.py:332
  179.8 0.9 copy-start.1
  180.7 0.9 copy-start.4
  181.6 8.6 %copy-start.6 = (bf16[1,16,1024]{2,1,0:T(8,128)(2,1)S(1)}, bf16[1,16,1024]{2,1,0:T(8,128)(2,1)}, u32[]{:S(2)}) copy-start(bf16[1,16,1024]{2,1,0:T(8,128)(2,1)} %param.10) | copy-start | bytes 98308
  191.6 11.1 %collective-permute-start.13 = (f32[16,768]{0,1:T(8,128)}, f32[16,768]{0,1:T(8,128)}, u32[]{:S(2)}, u32[]{:S(2)}) collective-permute-start(f32[16,768]{0,1:T(8,128)} %convolution_bitcast_fusion), channel_id=1, source_target_pairs={{0,1},{1,0},{2,3},{3,2},{4,5},{5,4},{6,7},{7,6},{8,9},{9,8},{10,11... | collective-permute-start | bytes 147464 | tf_op jit(solution)/shard_map/ppermute | solution.py:369
  203.8 14.2 %collective-permute-start.14 = (f32[16,768]{0,1:T(8,128)S(1)}, f32[16,768]{0,1:T(8,128)S(1)}, u32[]{:S(2)}, u32[]{:S(2)}) collective-permute-start(f32[16,768]{0,1:T(8,128)S(1)} %add.82), channel_id=1, source_target_pairs={{0,2},{1,3},{2,0},{3,1},{4,6},{5,7},{6,4},{7,5},{8,10},{9,11},{10,... | collective-permute-start | bytes 147464 | tf_op jit(solution)/shard_map/ppermute | solution.py:369
  205.2 18.1 %copy-start.2 = (bf16[768,128]{1,0:T(8,128)(2,1)S(1)}, bf16[768,128]{1,0:T(8,128)(2,1)}, u32[]{:S(2)}) copy-start(bf16[768,128]{1,0:T(8,128)(2,1)} %copy-done) | copy-start | bytes 589828
  205.2 18.1 %copy-start.5 = (bf16[768,128]{1,0:T(8,128)(2,1)S(1)}, bf16[768,128]{1,0:T(8,128)(2,1)}, u32[]{:S(2)}) copy-start(bf16[768,128]{1,0:T(8,128)(2,1)} %copy-done.3) | copy-start | bytes 589828
  218.1 11.0 %collective-permute-start.15 = (f32[16,768]{0,1:T(8,128)S(1)}, f32[16,768]{0,1:T(8,128)S(1)}, u32[]{:S(2)}, u32[]{:S(2)}) collective-permute-start(f32[16,768]{0,1:T(8,128)S(1)} %add.83), channel_id=1, source_target_pairs={{0,4},{1,5},{2,6},{3,7},{4,0},{5,1},{6,2},{7,3},{8,12},{9,13},{10,... | collective-permute-start | bytes 147464 | tf_op jit(solution)/shard_map/ppermute | solution.py:369
  230.3 45.6 %collective-permute-start.10 = (bf16[48,8192]{1,0:T(8,128)(2,1)S(1)}, bf16[48,8192]{1,0:T(8,128)(2,1)S(1)}, u32[]{:S(2)}, u32[]{:S(2)}) collective-permute-start(bf16[48,8192]{1,0:T(8,128)(2,1)S(1)} %slice.18), channel_id=1, source_target_pairs={{3,0},{0,1},{1,2},{2,3},{7,4},{4,5},{5,6},{6,7},{11,8},{8,9},{9,10... | collective-permute-start | bytes 2359304 | tf_op jit(solution)/shard_map/ppermute | solution.py:332
  232.8 43.2 %collective-permute-start.12 = (bf16[48,8192]{1,0:T(8,128)(2,1)S(1)}, bf16[48,8192]{1,0:T(8,128)(2,1)S(1)}, u32[]{:S(2)}, u32[]{:S(2)}) collective-permute-start(bf16[48,8192]{1,0:T(8,128)(2,1)S(1)} %slice.19), channel_id=1, source_target_pairs={{1,0},{2,1},{3,2},{0,3},{5,4},{6,5},{7,6},{4,7},{9,8},{10,9},{11,1... | collective-permute-start | bytes 2359304 | tf_op jit(solution)/shard_map/ppermute | solution.py:332
  236.0 39.9 %collective-permute-start.5 = (bf16[48,8192]{1,0:T(8,128)(2,1)S(1)}, bf16[48,8192]{1,0:T(8,128)(2,1)S(1)}, u32[]{:S(2)}, u32[]{:S(2)}) collective-permute-start(bf16[48,8192]{1,0:T(8,128)(2,1)S(1)} %slice.16), channel_id=1, source_target_pairs={{3,0},{0,1},{1,2},{2,3},{7,4},{4,5},{5,6},{6,7},{11,8},{8,9},{9,10... | collective-permute-start | bytes 2359304 | tf_op jit(solution)/shard_map/ppermute | solution.py:332
  237.3 38.6 %collective-permute-start.7 = (bf16[48,8192]{1,0:T(8,128)(2,1)S(1)}, bf16[48,8192]{1,0:T(8,128)(2,1)S(1)}, u32[]{:S(2)}, u32[]{:S(2)}) collective-permute-start(bf16[48,8192]{1,0:T(8,128)(2,1)S(1)} %slice.17), channel_id=1, source_target_pairs={{1,0},{2,1},{3,2},{0,3},{5,4},{6,5},{7,6},{4,7},{9,8},{10,9},{11,1... | collective-permute-start | bytes 2359304 | tf_op jit(solution)/shard_map/ppermute | solution.py:332

commit v2 on v1

--- a/solution.py
+++ b/solution.py
@@ -16,7 +16,7 @@
 F32 = jnp.float32
 BF16 = jnp.bfloat16
 HIGHEST = lax.Precision.HIGHEST
-VMEM_BYTES = 44 << 20
+VMEM_BYTES = 60 << 20
 
 NT = (((1,), (1,)), ((), ()))
 TN = (((0,), (0,)), ((), ()))
@@ -47,8 +47,9 @@
     return (position >= bounds[0:1]) & (position <= bounds[1:2])
 
 
-def forward_kernel(rows, q_ref, k_ref, v_ref, bounds_ref, ctx_ref, lse_ref):
-    start = window_start(pl.program_id(0), rows)
+def forward_kernel(rows, q_ref, k_ref, v_ref, bounds_ref, down_ref, ctx_ref, lse_ref, rank_ref, rank):
+    step = pl.program_id(0)
+    start = window_start(step, rows)
     keys = k_ref[pl.ds(start, KEYS), :]
     values = v_ref[pl.ds(start, KEYS), :]
     queries = stack_heads(q_ref[...])
@@ -59,12 +60,19 @@
     total = jnp.sum(expanded, axis=0, keepdims=True)
     probs = (expanded / total).astype(BF16)
     context = dot(values, probs, TN)
-    ctx_ref[...] = unstack_heads(context.T.astype(BF16), rows)
+    context = unstack_heads(context.T.astype(BF16), rows)
+    ctx_ref[...] = context
     lse_ref[0] = top + jnp.log2(total)
-
-
-def attention_forward(query, key, value, bounds):
+    rank[pl.ds(pl.multiple_of(step * rows, 32), rows), :] = dot(context, down_ref[...], NT)
+
+    @pl.when(step == pl.num_programs(0) - 1)
+    def _():
+        rank_ref[...] = rank[...].T
+
+
+def attention_forward(query, key, value, bounds, down):
     tokens, width = query.shape
+    ranks = down.shape[0]
     blocks, _, lanes = bounds.shape
     rows = tokens // blocks
     whole = pl.BlockSpec((tokens, HEAD), lambda i: (0, 0))
@@ -76,32 +84,35 @@
             whole,
             whole,
             pl.BlockSpec((1, 2, lanes), lambda i: (i, 0, 0)),
+            pl.BlockSpec((ranks, width), lambda i: (0, 0)),
         ],
         out_specs=[
             pl.BlockSpec((rows, width), lambda i: (i, 0)),
             pl.BlockSpec((1, 1, lanes), lambda i: (i, 0, 0)),
+            pl.BlockSpec((ranks, tokens), lambda i: (0, 0)),
         ],
         out_shape=[
             jax.ShapeDtypeStruct((tokens, width), BF16),
             jax.ShapeDtypeStruct((blocks, 1, lanes), F32),
+            jax.ShapeDtypeStruct((ranks, tokens), F32),
         ],
+        scratch_shapes=[pltpu.VMEM((tokens, ranks), F32)],
         compiler_params=pltpu.CompilerParams(vmem_limit_bytes=VMEM_BYTES),
-        cost_estimate=pl.CostEstimate(
-            flops=4 * tokens * KEYS * width,
-            bytes_accessed=4 * tokens * width,
-            transcendentals=blocks * KEYS * lanes,
-        ),
         name="attention_forward",
-    )(query, key, value, bounds)
-
-
-def project_kernel(parts, w_ref, up_ref, down_ref, *refs):
+    )(query, key, value, bounds, down)
+
+
+def project_kernel(last, parts, where_ref, member_ref, w_ref, up_ref, down_ref, *refs):
     x_refs = refs[:parts]
-    g_ref, rank_ref, acc, rank_acc = refs[parts:]
+    refs = refs[parts:]
+    if last:
+        context_ref, partial_ref, g_ref, rank_ref, map_ref, acc, rank_acc = refs
+    else:
+        g_ref, rank_ref, acc, rank_acc = refs
     step = pl.program_id(0)
     x = jnp.concatenate([r[...] for r in x_refs], axis=0)
-    product = dot(x, w_ref[...], NT)
-    rank = dot(x, up_ref[...], NT)
+    product = dot(w_ref[...], x, NT)
+    rank = dot(up_ref[0], x, NT)
 
     @pl.when(step == 0)
     def _():
@@ -113,44 +124,67 @@
         acc[...] += product
         rank_acc[...] += rank
 
+    if last:
+
+        @pl.when(step == member_ref[0])
+        def _():
+            total = up_map_terms(where_ref, context_ref, x_refs)
+            map_ref[...] = (partial_ref[...] + total) * (LORA_SCALE / math.sqrt(context_ref.shape[0]))
+
     @pl.when(step == pl.num_programs(0) - 1)
     def _():
-        projected = dot(rank_acc[...], down_ref[...].astype(F32), NN, HIGHEST)
-        g_ref[...] = (acc[...] + LORA_SCALE * projected).astype(BF16)
-        rank_ref[...] = rank_acc[...]
-
-
-def project(xs, weight, up, down):
+        projected = dot(down_ref[...].astype(F32), rank_acc[...], TN, HIGHEST)
+        g_ref[...] = (acc[...] + LORA_SCALE * projected).T.astype(BF16)
+        rank_ref[...] = rank_acc[...].T
+
+
+def up_map_terms(where_ref, context_ref, x_refs):
+    total = None
+    for index, ref in enumerate(x_refs):
+        count = ref.shape[0]
+        begin = pl.multiple_of(where_ref[index] * count, 32)
+        part = dot(context_ref[pl.ds(begin, count), :], ref[...].astype(F32), TN, HIGHEST)
+        total = part if total is None else total + part
+    return total
+
+
+def project(where, member, xs, weight, up, down, up_map_parts=None):
     features, depth = weight.shape
-    ranks = up.shape[0]
+    members, ranks, chunk = up.shape
     rows = sum(x.shape[0] for x in xs)
-    chunk = 1024
+    last = up_map_parts is not None
+    extra = list(up_map_parts) if last else []
+    whole = [pl.BlockSpec(e.shape, lambda i, w, m: (0, 0)) for e in extra]
+    out_specs = [
+        pl.BlockSpec((rows, features), lambda i, w, m: (0, 0)),
+        pl.BlockSpec((rows, ranks), lambda i, w, m: (0, 0)),
+    ]
+    out_shape = [
+        jax.ShapeDtypeStruct((rows, features), BF16),
+        jax.ShapeDtypeStruct((rows, ranks), F32),
+    ]
+    if last:
+        out_specs.append(pl.BlockSpec((ranks, chunk), lambda i, w, m: (0, 0)))
+        out_shape.append(jax.ShapeDtypeStruct((ranks, chunk), F32))
     return pl.pallas_call(
-        functools.partial(project_kernel, len(xs)),
-        grid=(depth // chunk,),
-        in_specs=[
-            pl.BlockSpec((features, chunk), lambda i: (0, i)),
-            pl.BlockSpec((ranks, chunk), lambda i: (0, i)),
-            pl.BlockSpec((ranks, features), lambda i: (0, 0)),
-        ]
-        + [pl.BlockSpec((x.shape[0], chunk), lambda i: (0, i)) for x in xs],
-        out_specs=[
-            pl.BlockSpec((rows, features), lambda i: (0, 0)),
-            pl.BlockSpec((rows, ranks), lambda i: (0, 0)),
-        ],
-        out_shape=[
-            jax.ShapeDtypeStruct((rows, features), BF16),
-            jax.ShapeDtypeStruct((rows, ranks), F32),
-        ],
-        scratch_shapes=[pltpu.VMEM((rows, features), F32), pltpu.VMEM((rows, ranks), F32)],
+        functools.partial(project_kernel, last, len(xs)),
+        grid_spec=pltpu.PrefetchScalarGridSpec(
+            num_scalar_prefetch=2,
+            grid=(members,),
+            in_specs=[
+                pl.BlockSpec((features, chunk), lambda i, w, m: (0, i)),
+                pl.BlockSpec((1, ranks, chunk), lambda i, w, m: (i, 0, 0)),
+                pl.BlockSpec((ranks, features), lambda i, w, m: (0, 0)),
+            ]
+            + [pl.BlockSpec((x.shape[0], chunk), lambda i, w, m: (0, i)) for x in xs]
+            + whole,
+            out_specs=out_specs,
+            scratch_shapes=[pltpu.VMEM((features, rows), F32), pltpu.VMEM((ranks, rows), F32)],
+        ),
+        out_shape=out_shape,
         compiler_params=pltpu.CompilerParams(vmem_limit_bytes=VMEM_BYTES),
-        cost_estimate=pl.CostEstimate(
-            flops=2 * rows * features * depth,
-            bytes_accessed=2 * features * depth + 2 * rows * depth,
-            transcendentals=0,
-        ),
         name="project",
-    )(weight, up, down, *xs)
+    )(where, member, weight, up, down, *xs, *extra)
 
 
 def backward_kernel(first, last, rows, where_ref, *refs):
@@ -254,45 +288,37 @@
         ],
         input_output_aliases=aliases,
         compiler_params=pltpu.CompilerParams(vmem_limit_bytes=VMEM_BYTES),
-        cost_estimate=pl.CostEstimate(
-            flops=10 * steps * rows * KEYS * width,
-            bytes_accessed=10 * steps * rows * width,
-            transcendentals=steps * KEYS * lanes,
-        ),
         name="attention_backward",
     )(where, *operands)
 
 
-def up_map_kernel(where_ref, member_ref, *refs):
-    rank_ref, x_ref, out_ref = refs[0], refs[1:-1], refs[-1]
-    rows = rank_ref.shape[0] // 8
-    total = None
-    offset = 0
-    for ref in x_ref:
-        count = ref.shape[0]
-        block, inner = offset // rows, offset % rows
-        begin = pl.multiple_of(where_ref[block] * rows + inner, 16)
-        part = dot(rank_ref[pl.ds(begin, count), :], ref[...].astype(F32), TN, HIGHEST)
-        total = part if total is None else total + part
-        offset += count
-    out_ref[...] = total * (LORA_SCALE / math.sqrt(rank_ref.shape[0]))
-
-
-def up_map(where, member, rank_context, xs, width):
-    tokens, ranks = rank_context.shape
+def up_map_kernel(where_ref, member_ref, gathered_ref, *refs):
+    x_refs, context_ref, out_ref = refs[:-2], refs[-2], refs[-1]
+    context_ref[...] = gathered_ref[...].T
+    out_ref[...] = up_map_terms(where_ref, context_ref, x_refs)
+
+
+def up_map(where, member, gathered, xs, width):
+    ranks, tokens = gathered.shape
     return pl.pallas_call(
         up_map_kernel,
         grid_spec=pltpu.PrefetchScalarGridSpec(
             num_scalar_prefetch=2,
             grid=(1,),
-            in_specs=[pl.BlockSpec((tokens, ranks), lambda i, w, m: (0, 0))]
+            in_specs=[pl.BlockSpec((ranks, tokens), lambda i, w, m: (0, 0))]
             + [pl.BlockSpec((x.shape[0], width), lambda i, w, m: (0, m[0])) for x in xs],
-            out_specs=pl.BlockSpec((ranks, width), lambda i, w, m: (0, 0)),
+            out_specs=[
+                pl.BlockSpec((tokens, ranks), lambda i, w, m: (0, 0)),
+                pl.BlockSpec((ranks, width), lambda i, w, m: (0, 0)),
+            ],
         ),
-        out_shape=jax.ShapeDtypeStruct((ranks, width), F32),
+        out_shape=[
+            jax.ShapeDtypeStruct((tokens, ranks), F32),
+            jax.ShapeDtypeStruct((ranks, width), F32),
+        ],
         compiler_params=pltpu.CompilerParams(vmem_limit_bytes=VMEM_BYTES),
         name="up_map",
-    )(where, member, rank_context, *xs)
+    )(where, member, gathered, *xs)
 
 
 def per_device(
@@ -312,7 +338,6 @@
     member = lax.axis_index("fsdp")
     shard = handoff_gradient[0]
     rows = shard.shape[0]
-    half = rows // 2
     tokens = rows * members
     heads = stored_queries.shape[2] // HEAD
 
@@ -334,20 +359,41 @@
     def mirrored(block):
         return lax.ppermute(block, "pipe", [(i, stages - 1 - i) for i in range(stages)])
 
+    def after(values, others):
+        return lax.optimization_barrier((tuple(values), tuple(others)))[0]
+
+    def exchanged(block, partner):
+        return lax.ppermute(block, "fsdp", [(f, f ^ partner) for f in range(members)])
+
+    def gather_small(block):
+        for bit, partner in enumerate((1, 2, ring)):
+            other = exchanged(block, partner)
+            low = (member >> bit) % 2 == 0
+            block = jnp.where(
+                low, jnp.concatenate([block, other]), jnp.concatenate([other, block])
+            )
+        return block
+
+    up_whole = gather_small(adapter_up)
+
+    down = adapter_down[0]
+    weight = output_weight[0]
+
     near = from_next(shard, 0)
-    across = from_next(shard, ring)
-    query = mirrored(stored_queries[0])
-    key = mirrored(stored_keys[0])
-    value = mirrored(stored_values[0])
-    up_whole = lax.all_gather(adapter_up[0], "fsdp", axis=1, tiled=True)
-    down = adapter_down[0]
-
     left0 = along_x(near, 1)
     right0 = along_x(near, -1)
-    left1 = along_x(across, 1)
-    right1 = along_x(across, -1)
-    far0 = (along_x(left0[:half], 1), along_x(right0[half:], -1))
-    far1 = (along_x(left1[:half], 1), along_x(right1[half:], -1))
+    second, parked_query, parked_key, parked_value = after(
+        (shard, stored_queries[0], stored_keys[0], stored_values[0]), (near,)
+    )
+    across = from_next(second, ring)
+    query = mirrored(parked_query)
+    key = mirrored(parked_key)
+    value = mirrored(parked_value)
+    far0 = along_x(left0, 1)
+    (across_later,) = after((across,), (left0, right0))
+    left1 = along_x(across_later, 1)
+    right1 = along_x(across_later, -1)
+    far1 = along_x(right1, -1)
 
     plane, x = member // ring, member % ring
 
@@ -360,43 +406,37 @@
     begin = jnp.sum((doc[None, :] < doc[:, None]).astype(jnp.int32), axis=1)
     bounds = jnp.stack([begin, position]).reshape(2, members, rows)
     bounds = jnp.tile(bounds.transpose(1, 0, 2), (1, 1, heads))
-
-    weight = output_weight[0]
-    context, lse = attention_forward(query, key, value, bounds)
-    rank_context = lax.dot_general(down, context, NT, preferred_element_type=F32)
-    for partner in (1, 2, ring):
-        route = [(f, f ^ partner) for f in range(members)]
-        rank_context = rank_context + lax.ppermute(rank_context, "fsdp", route)
+    me = member.reshape(1).astype(jnp.int32)
 
     groups = [
         (pair(0), [near, across]),
         (pair(-1), [left0, left1]),
         (pair(1), [right0, right1]),
-        (pair(2), [far0[0], far0[1], far1[0], far1[1]]),
     ]
+    projected = [project(where, me, xs, weight, up_whole, down) for where, xs in groups]
+    query, key, value = after((query, key, value), [g for g, _ in projected])
+    context, lse, rank_part = attention_forward(query, key, value, bounds, down)
+    for partner in (1, 2, ring):
+        rank_part = rank_part + exchanged(rank_part, partner)
     carried = None
-    for number, (where, xs) in enumerate(groups):
-        gradient, rank = project(xs, weight, up_whole, down)
+    for (where, _), (gradient, rank) in zip(groups, projected):
         carried = attention_backward(
-            where,
-            query,
-            context,
-            lse,
-            bounds,
-            gradient,
-            rank,
-            key,
-            value,
-            carried,
-            number == len(groups) - 1,
+            where, query, context, lse, bounds, gradient, rank, key, value, carried, False
         )
-    query_gradient, key_gradient, value_gradient, down_map_gradient = carried
-    up_map_gradient = up_map(
+    rank_context, partial = up_map(
         jnp.concatenate([where for where, _ in groups]),
-        member.reshape(1).astype(jnp.int32),
-        rank_context.T,
+        me,
+        rank_part,
         [x for _, xs in groups for x in xs],
         adapter_up.shape[2],
+    )
+    where = pair(2)
+    far0, far1 = after((far0, far1), (carried[3], partial))
+    gradient, rank, up_map_gradient = project(
+        where, me, [far0, far1], weight, up_whole, down, (rank_context, partial)
+    )
+    query_gradient, key_gradient, value_gradient, down_map_gradient = attention_backward(
+        where, query, context, lse, bounds, gradient, rank, key, value, carried, True
     )
     return (
         query_gradient[None],

time: 299 us -> 272 us (0.910)
  blocking collectives: 91.3 us -> 0 us
  waiting for transfers between devices: 78.7 us -> 123 us
  Pallas kernels: 82.8 us -> 102 us
  local copies, waits for them, and re-layouts: 6.9 us -> 2.76 us
  other arithmetic: 2.64 us -> 6.5 us
    all_gather x1 -> x0, blocking collectives: 91.3 us -> none  [per_device(): up_whole = lax.all_gather(adapter_up[0], 'fsdp', axis=1, tiled=True)]
    ppermute x8 -> x6, waiting for transfers between devices: 0.02 us -> 37.7 us  [along_x(): return lax.ppermute(block, 'fsdp', route)]
    ppermute x3 -> x6, waiting for transfers between devices: 10.1 us -> 42.1 us  [exchanged(): lax.ppermute(block, 'fsdp', [(f, f ^ partner) for f in range(members)])]
    ppermute x2, waiting for transfers between devices: 68.6 us -> 43.2 us  [from_next(): return lax.ppermute(block, both, route)]
    pallas_call x4, Pallas kernels: 51.1 us -> 59.6 us  [project(): pl.pallas_call(functools.partial(project_kernel, last, len(xs)), grid_spe...]
    pallas_call x4, Pallas kernels: 19.1 us -> 27 us  [attention_backward(): pl.pallas_call(functools.partial(backward_kernel, first, last, rows), gri...]
    slice x4 -> x0, local copies, waits for them, and re-layouts: 4.74 us -> none  [the longest x2 2.37 us: per_device(): far0 = (along_x(left0[:half], 1), along_x(right0[half:], -1))]
    ppermute x8 -> x6, starting transfers between devices: 13.4 us -> 9.97 us  [along_x(): return lax.ppermute(block, 'fsdp', route)]
  transfers between devices with their start and end apart: 16 -> 17, of which waited for: 3 -> 10; matrix products, arithmetic and copies ran while one was open for 3% -> 3% of each run, Pallas kernels for 21% -> 30%
where the time goes in v2:
time: 272 us; the launch traced here: 269 us
  waiting for transfers between devices  123 us (45%)
  Pallas kernels  102 us (38%)
  starting transfers between devices  33.5 us (12%)
  other arithmetic  6.5 us (2%)
  local copies, waits for them, and re-layouts  2.76 us (1%)
    pallas_call x4, Pallas kernels, project(): pl.pallas_call(functools.partial(project_kernel, last, len(xs)), grid_spe...  59.6 us
    ppermute x2, waiting for transfers between devices, from_next(): return lax.ppermute(block, both, route)  43.2 us
    ppermute x6, waiting for transfers between devices, exchanged(): lax.ppermute(block, 'fsdp', [(f, f ^ partner) for f in range(members)])  42.1 us
    ppermute x6, waiting for transfers between devices, along_x(): return lax.ppermute(block, 'fsdp', route)  37.7 us
    pallas_call x4, Pallas kernels, attention_backward(): pl.pallas_call(functools.partial(backward_kernel, first, last, rows), gri...  27 us
    pallas_call x1, Pallas kernels, attention_forward(): pl.pallas_call(functools.partial(forward_kernel, rows), grid=(blocks,), i...  11.8 us
    ppermute x2, starting transfers between devices, from_next(): return lax.ppermute(block, both, route)  10.1 us
    ppermute x6, starting transfers between devices, along_x(): return lax.ppermute(block, 'fsdp', route)  9.97 us
  transfers between devices with their start and end apart: 17, of which 10 were waited for; matrix products, arithmetic and copies ran while one was open for 3% of the time, Pallas kernels for 30%

profile of v2, /device:TPU:0, one launch (start us, length us, event | category | flops | bytes accessed | tf_op | source)
XLA Modules:
  0.0 268.9 jit_solution(18231107192265755230)
XLA Ops:
  0.6 4.0 %collective-permute-start = (bf16[96,8192]{1,0:T(8,128)(2,1)}, bf16[96,8192]{1,0:T(8,128)(2,1)S(1)}, u32[]{:S(2)}, u32[]{:S(2)}) collective-permute-start(bf16[96,8192]{1,0:T(8,128)(2,1)} %bitcast.34), channel_id=1, source_target_pairs={{8,0},{9,1},{10,2},{11,3},{12,4},{13,5},{14,6},{15,7},{16,8},{17,9... | collective-permute-start | bytes 4718600 | tf_op jit(solution)/shard_map/ppermute | solution.py:350
  4.6 18.3 %collective-permute-done.refs_0_ = bf16[96,8192]{1,0:T(8,128)(2,1)S(1)} collective-permute-done((bf16[96,8192]{1,0:T(8,128)(2,1)}, bf16[96,8192]{1,0:T(8,128)(2,1)S(1)}, u32[]{:S(2)}, u32[]{:S(2)}) %collective-permute-start) | collective-permute-done | bytes 1572896 | tf_op jit(solution)/shard_map/ppermute | solution.py:350
  22.8 6.1 %collective-permute-start.7 = (bf16[96,8192]{1,0:T(8,128)(2,1)}, bf16[96,8192]{1,0:T(8,128)(2,1)}, u32[]{:S(2)}, u32[]{:S(2)}) collective-permute-start(bf16[96,8192]{1,0:T(8,128)(2,1)} %bitcast.35), channel_id=1, source_target_pairs={{12,0},{13,1},{14,2},{15,3},{8,4},{9,5},{10,6},{11,7},{20,8},{21,9... | collective-permute-start | bytes 4718600 | tf_op jit(solution)/shard_map/ppermute | solution.py:350
  28.9 1.5 collective-permute-start.8
  30.4 1.7 collective-permute-start.9
  32.2 24.9 %collective-permute-done.7.refs_1_ = bf16[96,8192]{1,0:T(8,128)(2,1)} collective-permute-done((bf16[96,8192]{1,0:T(8,128)(2,1)}, bf16[96,8192]{1,0:T(8,128)(2,1)}, u32[]{:S(2)}, u32[]{:S(2)}) %collective-permute-start.7) | collective-permute-done | bytes 1572896 | tf_op jit(solution)/shard_map/ppermute | solution.py:350
  57.1 7.0 %collective-permute-done.8.refs_0_.refs_2_ = bf16[96,8192]{1,0:T(8,128)(2,1)} collective-permute-done((bf16[96,8192]{1,0:T(8,128)(2,1)S(1)}, bf16[96,8192]{1,0:T(8,128)(2,1)}, u32[]{:S(2)}, u32[]{:S(2)}) %collective-permute-start.8) | collective-permute-done | bytes 1572896 | tf_op jit(solution)/shard_map/ppermute | solution.py:357
  64.2 0.2 collective-permute-done.9.refs_0_.refs_4_
  64.4 2.6 collective-permute-start.11
  67.0 0.0 copy-done.2
  67.0 0.3 collective-permute-start.10
  67.3 0.0 collective-permute-start.1
  67.3 1.2 collective-permute-start.12
  68.5 30.4 %collective-permute-done.11.refs_1_.refs_5_ = bf16[96,8192]{1,0:T(8,128)(2,1)} collective-permute-done((bf16[96,8192]{1,0:T(8,128)(2,1)}, bf16[96,8192]{1,0:T(8,128)(2,1)}, u32[]{:S(2)}, u32[]{:S(2)}) %collective-permute-start.11) | collective-permute-done | bytes 1572896 | tf_op jit(solution)/shard_map/ppermute | solution.py:357
  99.0 2.6 collective-permute-start.13
  101.6 0.0 collective-permute-start.4
  101.6 0.7 reduce
  102.3 0.4 convert_reduce_fusion
  102.7 0.1 stack.61
  102.8 29.9 %collective-permute-done.4 = bf16[1,16,1024]{2,1,0:T(8,128)(2,1)S(1)} collective-permute-done((bf16[1,16,1024]{2,1,0:T(8,128)(2,1)}, bf16[1,16,1024]{2,1,0:T(8,128)(2,1)S(1)}, u32[]{:S(2)}, u32[]{:S(2)}) %collective-permute-start.4) | collective-permute-done | bytes 32800 | tf_op jit(solution)/shard_map/ppermute | solution.py:366
  132.7 0.8 maximum_select_fusion.2
  133.5 2.7 collective-permute-start.5
  136.2 3.2 %collective-permute-done.5 = bf16[2,16,1024]{2,1,0:T(8,128)(2,1)S(1)} collective-permute-done((bf16[2,16,1024]{2,1,0:T(8,128)(2,1)S(1)}, bf16[2,16,1024]{2,1,0:T(8,128)(2,1)S(1)}, u32[]{:S(2)}, u32[]{:S(2)}) %collective-permute-start.5) | collective-permute-done | bytes 65568 | tf_op jit(solution)/shard_map/ppermute | solution.py:366
  139.4 0.8 collective-permute-start.6
  140.2 0.6 pad_add_fusion.3.where_ref
  140.8 0.7 tile.10.bounds_ref.refs_3_
  141.6 0.6 pad_add_fusion.2.where_ref
  142.1 3.8 %collective-permute-done.6 = bf16[4,16,1024]{2,1,0:T(8,128)(2,1)S(1)} collective-permute-done((bf16[4,16,1024]{2,1,0:T(8,128)(2,1)S(1)}, bf16[4,16,1024]{2,1,0:T(8,128)(2,1)S(1)}, u32[]{:S(2)}, u32[]{:S(2)}) %collective-permute-start.6) | collective-permute-done | bytes 131104 | tf_op jit(solution)/shard_map/ppermute | solution.py:366
  145.9 0.5 collective-permute-start.2
  146.5 0.0 collective-permute-done.10.refs_1_.refs_3_
  146.5 3.3 %collective-permute-start.3 = (bf16[768,128]{1,0:T(8,128)(2,1)}, bf16[768,128]{1,0:T(8,128)(2,1)S(1)}, u32[]{:S(2)}, u32[]{:S(2)}) collective-permute-start(bf16[768,128]{1,0:T(8,128)(2,1)} %bitcast.38), channel_id=1, source_target_pairs={{0,120},{8,112},{16,104},{24,96},{32,88},{40,80},{48,72},{56,64},{... | collective-permute-start | bytes 589832 | tf_op jit(solution)/shard_map/ppermute | solution.py:360
  149.8 0.6 pad_add_fusion.1.where_ref
  150.4 0.7 maximum_select_fusion.up_ref
  151.1 0.0 copy-done.1
  151.1 14.8 %project.4 = (bf16[192,1024]{1,0:T(8,128)(2,1)}, f32[192,16]{1,0:T(8,128)}) custom-call(s32[2]{0:T(128)} %pad_add_fusion.1.where_ref, s32[1]{0:T(128)} %bitcast.8.member_ref, bf16[1024,8192]{1,0:T(8,128)(2,1)} %bitcast.24, bf16[8,16,1024]{2,1,0:T(8,128)(2,1)} %maximum_select_fusion.up_ref, bf16[16,1024]{1,0:T(8,128)(2,1)} %bitcast.29, ...), custom_call_target="tpu_custom_call" | custom-call | tf_op jit(solution)/shard_map/project/pallas_call | solution.py:169
  166.0 14.8 %project.6 = (bf16[192,1024]{1,0:T(8,128)(2,1)}, f32[192,16]{1,0:T(8,128)}) custom-call(s32[2]{0:T(128)} %pad_add_fusion.3.where_ref, s32[1]{0:T(128)} %bitcast.8.member_ref, bf16[1024,8192]{1,0:T(8,128)(2,1)} %bitcast.25, bf16[8,16,1024]{2,1,0:T(8,128)(2,1)} %maximum_select_fusion.up_ref, bf16[16,1024]{1,0:T(8,128)(2,1)} %bitcast.30, ...), custom_call_target="tpu_custom_call" | custom-call | tf_op jit(solution)/shard_map/project/pallas_call | solution.py:169
  180.8 14.8 %project.5 = (bf16[192,1024]{1,0:T(8,128)(2,1)}, f32[192,16]{1,0:T(8,128)}) custom-call(s32[2]{0:T(128)} %pad_add_fusion.2.where_ref, s32[1]{0:T(128)} %bitcast.8.member_ref, bf16[1024,8192]{1,0:T(8,128)(2,1)} %bitcast.26, bf16[8,16,1024]{2,1,0:T(8,128)(2,1)} %maximum_select_fusion.up_ref, bf16[16,1024]{1,0:T(8,128)(2,1)} %bitcast.31, ...), custom_call_target="tpu_custom_call" | custom-call | tf_op jit(solution)/shard_map/project/pallas_call | solution.py:169
  195.6 0.0 collective-permute-done.2.k_ref.refs_6_
  195.6 0.0 collective-permute-done.3.v_ref.refs_7_
  195.6 0.0 copy-start.4
  195.6 0.0 collective-permute-done.1.q_ref.refs_0_
  195.6 0.0 copy-start
  195.6 0.6 copy-done.3
  196.3 0.1 copy-done.4
  196.3 0.6 copy-done
  196.9 11.8 %attention_forward.1 = (bf16[768,1024]{1,0:T(8,128)(2,1)}, f32[8,1,768]{2,1,0:T(1,128)}, f32[16,768]{1,0:T(8,128)}) custom-call(bf16[768,1024]{1,0:T(8,128)(2,1)} %copy-done, bf16[768,128]{1,0:T(8,128)(2,1)} %copy-done.3, bf16[768,128]{1,0:T(8,128)(2,1)} %copy-done.4, s32[8,2,768]{2,1,0:T(2,128)} %tile.10.bounds_ref.refs_3_, bf16[16,1024]{1,0:T(8,128)(2,1)} %bitcast.32), custom_call_target="tpu_custom_call" | custom-call | tf_op jit(solution)/shard_map/attention_forward/pallas_call | solution.py:79
  208.7 2.4 collective-permute-start.14
  211.1 2.3 collective-permute-done.14
  213.4 0.8 add.94
  214.2 2.7 collective-permute-start.15
  216.8 2.9 %collective-permute-done.15 = f32[16,768]{1,0:T(8,128)S(1)} collective-permute-done((f32[16,768]{1,0:T(8,128)S(1)}, f32[16,768]{1,0:T(8,128)S(1)}, u32[]{:S(2)}, u32[]{:S(2)}) %collective-permute-start.15) | collective-permute-done | bytes 49184 | tf_op jit(solution)/shard_map/ppermute | solution.py:366
  219.8 1.1 collective-permute-start.16
  220.8 0.6 pad_add_fusion.where_ref
  221.5 0.7 concatenate.29.where_ref
  222.1 6.6 %attention_backward.4 = (bf16[768,1024]{1,0:T(8,128)(2,1)}, f32[768,128]{1,0:T(8,128)}, f32[768,128]{1,0:T(8,128)}, f32[16,1024]{1,0:T(8,128)}) custom-call(s32[2]{0:T(128)} %pad_add_fusion.1.where_ref, bf16[768,1024]{1,0:T(8,128)(2,1)} %copy-done, bf16[768,1024]{1,0:T(8,128)(2,1)} %get-tuple-element.56.refs_1_, f32[8,1,768]{2,1,0:T(1,128)} %get-tuple-element.57.refs_2_, ...), custom_call_target="tpu_custom_call" | custom-call | tf_op jit(solution)/shard_map/attention_backward/pallas_call | solution.py:270
  228.7 6.8 %attention_backward.5 = (bf16[768,1024]{1,0:T(8,128)(2,1)}, f32[768,128]{1,0:T(8,128)}, f32[768,128]{1,0:T(8,128)}, f32[16,1024]{1,0:T(8,128)}) custom-call(s32[2]{0:T(128)} %pad_add_fusion.2.where_ref, bf16[768,1024]{1,0:T(8,128)(2,1)} %copy-done, bf16[768,1024]{1,0:T(8,128)(2,1)} %get-tuple-element.56.refs_1_, ...), custom_call_target="tpu_custom_call", output_to_operand_aliasing={{0}: (9, {})} | custom-call | tf_op jit(solution)/shard_map/attention_backward/pallas_call | solution.py:270
  235.6 6.9 %attention_backward.6 = (bf16[768,1024]{1,0:T(8,128)(2,1)}, f32[768,128]{1,0:T(8,128)}, f32[768,128]{1,0:T(8,128)}, f32[16,1024]{1,0:T(8,128)}) custom-call(s32[2]{0:T(128)} %pad_add_fusion.3.where_ref, bf16[768,1024]{1,0:T(8,128)(2,1)} %copy-done, bf16[768,1024]{1,0:T(8,128)(2,1)} %get-tuple-element.56.refs_1_, ...), custom_call_target="tpu_custom_call", output_to_operand_aliasing={{0}: (9, {})} | custom-call | tf_op jit(solution)/shard_map/attention_backward/pallas_call | solution.py:270
  242.4 0.0 collective-permute-done.16
  242.4 0.6 add.96.gathered_ref
  243.0 3.9 %up_map.1 = (f32[768,16]{1,0:T(8,128)}, f32[16,1024]{1,0:T(8,128)}) custom-call(s32[6]{0:T(128)} %concatenate.29.where_ref, s32[1]{0:T(128)} %bitcast.8.member_ref, f32[16,768]{1,0:T(8,128)} %add.96.gathered_ref, bf16[96,8192]{1,0:T(8,128)(2,1)} %copy-done.1, bf16[96,8192]{1,0:T(8,128)(2,1)} %collective-permute-done.7.refs_1_, ...), custom_call_target="tpu_custom_call" | custom-call | tf_op jit(solution)/shard_map/up_map/pallas_call | solution.py:303
  247.0 0.0 collective-permute-done.12.refs_0_
  247.0 0.0 collective-permute-done.13.refs_1_
  247.0 15.1 %project.7 = (bf16[192,1024]{1,0:T(8,128)(2,1)}, f32[192,16]{1,0:T(8,128)}, f32[16,1024]{1,0:T(8,128)}) custom-call(s32[2]{0:T(128)} %pad_add_fusion.where_ref, s32[1]{0:T(128)} %bitcast.8.member_ref, bf16[1024,8192]{1,0:T(8,128)(2,1)} %bitcast.27, bf16[8,16,1024]{2,1,0:T(8,128)(2,1)} %maximum_select_fusion.up_ref, bf16[16,1024]{1,0:T(8,128)(2,1)} %bitcast.33, ...), custom_call_target="tpu_custom_call" | custom-call | tf_op jit(solution)/shard_map/project/pallas_call | solution.py:169
  262.1 6.7 %attention_backward.7 = (bf16[768,1024]{1,0:T(8,128)(2,1)}, bf16[768,128]{1,0:T(8,128)(2,1)}, bf16[768,128]{1,0:T(8,128)(2,1)}, f32[16,1024]{1,0:T(8,128)}) custom-call(s32[2]{0:T(128)} %pad_add_fusion.where_ref, bf16[768,1024]{1,0:T(8,128)(2,1)} %copy-done, bf16[768,1024]{1,0:T(8,128)(2,1)} %get-tuple-element.56.refs_1_, ...), custom_call_target="tpu_custom_call", output_to_operand_aliasing={{0}: (9, {})} | custom-call | tf_op jit(solution)/shard_map/attention_backward/pallas_call | solution.py:270
  (8 shorter events, 0.1 us)
Async XLA Ops:
  0.6 22.2 %collective-permute-start = (bf16[96,8192]{1,0:T(8,128)(2,1)}, bf16[96,8192]{1,0:T(8,128)(2,1)S(1)}, u32[]{:S(2)}, u32[]{:S(2)}) collective-permute-start(bf16[96,8192]{1,0:T(8,128)(2,1)} %bitcast.34), channel_id=1, source_target_pairs={{8,0},{9,1},{10,2},{11,3},{12,4},{13,5},{14,6},{15,7},{16,8},{17,9... | collective-permute-start | bytes 4718600 | tf_op jit(solution)/shard_map/ppermute | solution.py:350
  22.8 128.3 %copy-start.1 = (bf16[96,8192]{1,0:T(8,128)(2,1)}, bf16[96,8192]{1,0:T(8,128)(2,1)S(1)}, u32[]{:S(2)}) copy-start(bf16[96,8192]{1,0:T(8,128)(2,1)S(1)} %collective-permute-done.refs_0_) | copy-start | bytes 4718596
  22.8 34.3 %collective-permute-start.7 = (bf16[96,8192]{1,0:T(8,128)(2,1)}, bf16[96,8192]{1,0:T(8,128)(2,1)}, u32[]{:S(2)}, u32[]{:S(2)}) collective-permute-start(bf16[96,8192]{1,0:T(8,128)(2,1)} %bitcast.35), channel_id=1, source_target_pairs={{12,0},{13,1},{14,2},{15,3},{8,4},{9,5},{10,6},{11,7},{20,8},{21,9... | collective-permute-start | bytes 4718600 | tf_op jit(solution)/shard_map/ppermute | solution.py:350
  28.9 35.2 %collective-permute-start.8 = (bf16[96,8192]{1,0:T(8,128)(2,1)S(1)}, bf16[96,8192]{1,0:T(8,128)(2,1)}, u32[]{:S(2)}, u32[]{:S(2)}) collective-permute-start(bf16[96,8192]{1,0:T(8,128)(2,1)S(1)} %collective-permute-done.refs_0_), channel_id=1, source_target_pairs={{3,0},{0,1},{1,2},{2,3},{7,4},{4,5},{5,6},{6,7},{11,8},{8,9},{9,10... | collective-permute-start | bytes 4718600 | tf_op jit(solution)/shard_map/ppermute | solution.py:357
  30.4 34.0 %collective-permute-start.9 = (bf16[96,8192]{1,0:T(8,128)(2,1)S(1)}, bf16[96,8192]{1,0:T(8,128)(2,1)S(1)}, u32[]{:S(2)}, u32[]{:S(2)}) collective-permute-start(bf16[96,8192]{1,0:T(8,128)(2,1)S(1)} %collective-permute-done.refs_0_), channel_id=1, source_target_pairs={{1,0},{2,1},{3,2},{0,3},{5,4},{6,5},{7,6},{4,7},{9,8},{10,9},{11,1... | collective-permute-start | bytes 4718600 | tf_op jit(solution)/shard_map/ppermute | solution.py:357
  64.4 2.6 copy-start.2
  64.4 34.6 %collective-permute-start.11 = (bf16[96,8192]{1,0:T(8,128)(2,1)}, bf16[96,8192]{1,0:T(8,128)(2,1)}, u32[]{:S(2)}, u32[]{:S(2)}) collective-permute-start(bf16[96,8192]{1,0:T(8,128)(2,1)} %collective-permute-done.7.refs_1_), channel_id=1, source_target_pairs={{1,0},{2,1},{3,2},{0,3},{5,4},{6,5},{7,6},{4,7},{9,8},{10,9},{11,1... | collective-permute-start | bytes 4718600 | tf_op jit(solution)/shard_map/ppermute | solution.py:357
  67.0 79.5 %collective-permute-start.10 = (bf16[96,8192]{1,0:T(8,128)(2,1)}, bf16[96,8192]{1,0:T(8,128)(2,1)}, u32[]{:S(2)}, u32[]{:S(2)}) collective-permute-start(bf16[96,8192]{1,0:T(8,128)(2,1)} %collective-permute-done.7.refs_1_), channel_id=1, source_target_pairs={{3,0},{0,1},{1,2},{2,3},{7,4},{4,5},{5,6},{6,7},{11,8},{8,9},{9,10... | collective-permute-start | bytes 4718600 | tf_op jit(solution)/shard_map/ppermute | solution.py:357
  67.3 128.3 %collective-permute-start.1 = (bf16[768,1024]{1,0:T(8,128)(2,1)}, bf16[768,1024]{1,0:T(8,128)(2,1)S(1)}, u32[]{:S(2)}, u32[]{:S(2)}) collective-permute-start(bf16[768,1024]{1,0:T(8,128)(2,1)} %bitcast.36), channel_id=1, source_target_pairs={{0,120},{8,112},{16,104},{24,96},{32,88},{40,80},{48,72},{56,64},{... | collective-permute-start | bytes 4718600 | tf_op jit(solution)/shard_map/ppermute | solution.py:360
  67.3 179.7 %collective-permute-start.12 = (bf16[96,8192]{1,0:T(8,128)(2,1)}, bf16[96,8192]{1,0:T(8,128)(2,1)}, u32[]{:S(2)}, u32[]{:S(2)}) collective-permute-start(bf16[96,8192]{1,0:T(8,128)(2,1)} %collective-permute-done.8.refs_0_.refs_2_), channel_id=1, source_target_pairs={{3,0},{0,1},{1,2},{2,3},{7,4},{4,5},{5,6},{6,7},{11,8},{8,9},{9,10... | collective-permute-start | bytes 4718600 | tf_op jit(solution)/shard_map/ppermute | solution.py:357
  99.0 148.0 %collective-permute-start.13 = (bf16[96,8192]{1,0:T(8,128)(2,1)}, bf16[96,8192]{1,0:T(8,128)(2,1)}, u32[]{:S(2)}, u32[]{:S(2)}) collective-permute-start(bf16[96,8192]{1,0:T(8,128)(2,1)} %collective-permute-done.11.refs_1_.refs_5_), channel_id=1, source_target_pairs={{1,0},{2,1},{3,2},{0,3},{5,4},{6,5},{7,6},{4,7},{9,8},{10,9},{11,1... | collective-permute-start | bytes 4718600 | tf_op jit(solution)/shard_map/ppermute | solution.py:357
  101.6 31.1 %collective-permute-start.4 = (bf16[1,16,1024]{2,1,0:T(8,128)(2,1)}, bf16[1,16,1024]{2,1,0:T(8,128)(2,1)S(1)}, u32[]{:S(2)}, u32[]{:S(2)}) collective-permute-start(bf16[1,16,1024]{2,1,0:T(8,128)(2,1)} %param.11), channel_id=1, source_target_pairs={{0,1},{1,0},{2,3},{3,2},{4,5},{5,4},{6,7},{7,6},{8,9},{9,8},{10,11... | collective-permute-start | bytes 98312 | tf_op jit(solution)/shard_map/ppermute | solution.py:366
  133.5 5.8 %collective-permute-start.5 = (bf16[2,16,1024]{2,1,0:T(8,128)(2,1)S(1)}, bf16[2,16,1024]{2,1,0:T(8,128)(2,1)S(1)}, u32[]{:S(2)}, u32[]{:S(2)}) collective-permute-start(bf16[2,16,1024]{2,1,0:T(8,128)(2,1)S(1)} %maximum_select_fusion.2), channel_id=1, source_target_pairs={{0,2},{1,3},{2,0},{3,1},{4,6},{5,7},{6,4},{7,5},{8,10},{9,11},{10,... | collective-permute-start | bytes 196616 | tf_op jit(solution)/shard_map/ppermute | solution.py:366
  139.4 6.6 %collective-permute-start.6 = (bf16[4,16,1024]{2,1,0:T(8,128)(2,1)S(1)}, bf16[4,16,1024]{2,1,0:T(8,128)(2,1)S(1)}, u32[]{:S(2)}, u32[]{:S(2)}) collective-permute-start(bf16[4,16,1024]{2,1,0:T(8,128)(2,1)S(1)} %maximum_select_fusion.1), channel_id=1, source_target_pairs={{0,4},{1,5},{2,6},{3,7},{4,0},{5,1},{6,2},{7,3},{8,12},{9,13},{10,... | collective-permute-start | bytes 393224 | tf_op jit(solution)/shard_map/ppermute | solution.py:366
  145.9 49.6 %collective-permute-start.2 = (bf16[768,128]{1,0:T(8,128)(2,1)}, bf16[768,128]{1,0:T(8,128)(2,1)S(1)}, u32[]{:S(2)}, u32[]{:S(2)}) collective-permute-start(bf16[768,128]{1,0:T(8,128)(2,1)} %bitcast.37), channel_id=1, source_target_pairs={{0,120},{8,112},{16,104},{24,96},{32,88},{40,80},{48,72},{56,64},{... | collective-permute-start | bytes 589832 | tf_op jit(solution)/shard_map/ppermute | solution.py:360
  146.5 49.1 %collective-permute-start.3 = (bf16[768,128]{1,0:T(8,128)(2,1)}, bf16[768,128]{1,0:T(8,128)(2,1)S(1)}, u32[]{:S(2)}, u32[]{:S(2)}) collective-permute-start(bf16[768,128]{1,0:T(8,128)(2,1)} %bitcast.38), channel_id=1, source_target_pairs={{0,120},{8,112},{16,104},{24,96},{32,88},{40,80},{48,72},{56,64},{... | collective-permute-start | bytes 589832 | tf_op jit(solution)/shard_map/ppermute | solution.py:360
  195.6 0.7 copy-start.3
  195.6 0.7 copy-start.4
  195.6 1.3 copy-start
  208.7 4.7 %collective-permute-start.14 = (f32[16,768]{1,0:T(8,128)}, f32[16,768]{1,0:T(8,128)S(1)}, u32[]{:S(2)}, u32[]{:S(2)}) collective-permute-start(f32[16,768]{1,0:T(8,128)} %get-tuple-element.70), channel_id=1, source_target_pairs={{0,1},{1,0},{2,3},{3,2},{4,5},{5,4},{6,7},{7,6},{8,9},{9,8},{10,11... | collective-permute-start | bytes 147464 | tf_op jit(solution)/shard_map/ppermute | solution.py:366
  214.2 5.6 %collective-permute-start.15 = (f32[16,768]{1,0:T(8,128)S(1)}, f32[16,768]{1,0:T(8,128)S(1)}, u32[]{:S(2)}, u32[]{:S(2)}) collective-permute-start(f32[16,768]{1,0:T(8,128)S(1)} %add.94), channel_id=1, source_target_pairs={{0,2},{1,3},{2,0},{3,1},{4,6},{5,7},{6,4},{7,5},{8,10},{9,11},{10,... | collective-permute-start | bytes 147464 | tf_op jit(solution)/shard_map/ppermute | solution.py:366
  219.8 22.6 %collective-permute-start.16 = (f32[16,768]{1,0:T(8,128)S(1)}, f32[16,768]{1,0:T(8,128)S(1)}, u32[]{:S(2)}, u32[]{:S(2)}) collective-permute-start(f32[16,768]{1,0:T(8,128)S(1)} %add.95), channel_id=1, source_target_pairs={{0,4},{1,5},{2,6},{3,7},{4,0},{5,1},{6,2},{7,3},{8,12},{9,13},{10,... | collective-permute-start | bytes 147464 | tf_op jit(solution)/shard_map/ppermute | solution.py:366

commit v3 on v0

v3 whole, which is shorter than its diff:
```python
import functools
import math

import jax
import jax.numpy as jnp
from jax import lax
from jax.experimental import pallas as pl
from jax.experimental.pallas import tpu as pltpu
from jax.sharding import PartitionSpec as P

HEAD = 128
KEYS = 512
CHUNKS = 4
LORA_SCALE = 2.0
NEG = -1e30
LOG2E = math.log2(math.e)
F32 = jnp.float32
BF16 = jnp.bfloat16
HIGHEST = lax.Precision.HIGHEST
MESH = pl.DeviceIdType.MESH
VMEM_BYTES = 60 << 20

NT = (((1,), (1,)), ((), ()))
TN = (((0,), (0,)), ((), ()))
NN = (((1,), (0,)), ((), ()))

NEAR, ACROSS, RIGHT0, RIGHT1, FAR0, FAR1, LEFT0, LEFT1 = range(8)


def dot(a, b, dims, precision=None):
    return lax.dot_general(a, b, dims, precision=precision, preferred_element_type=F32)


def stack_heads(rows):
    heads = rows.shape[1] // HEAD
    return jnp.concatenate([rows[:, h * HEAD : (h + 1) * HEAD] for h in range(heads)], axis=0)


def unstack_heads(stacked, count):
    heads = stacked.shape[0] // count
    return jnp.concatenate([stacked[h * count : (h + 1) * count] for h in range(heads)], axis=1)


def kernel(
    stages,
    members,
    shard,
    weight_hbm,
    down,
    up_hbm,
    query_hbm,
    key_hbm,
    value_hbm,
    segments,
    dq_ref,
    dk_ref,
    dv_ref,
    down_map_ref,
    up_map_ref,
    x_ref,
    weight,
    up,
    query,
    key,
    value,
    doc,
    context,
    lse,
    gradient,
    rank,
    acc,
    rank_acc,
    dq,
    dk,
    dv,
    rank_context,
    rank_sum,
    rank_parts,
    shard_send,
    shard_recv,
    parked_send,
    parked_recv,
    up_send,
    up_recv,
    rank_send,
    rank_recv,
    weight_sem,
    up_sem,
    dq_sem,
):
    pipe = lax.axis_index("pipe")
    member = lax.axis_index("fsdp")
    ring = members // 2
    plane, x = member // ring, member % ring
    rows, depth = shard.shape
    tokens, width = query_hbm.shape
    heads = width // HEAD
    ranks = down.shape[0]
    lanes = heads * rows
    wide = depth // CHUNKS
    local = depth // members
    before = (pipe + stages - 1) % stages
    behind = (pipe + 1) % stages
    flipped = (member + ring) % members
    to_left = plane * ring + (x + ring - 1) % ring
    to_right = plane * ring + (x + 1) % ring

    def device(p, f):
        return {"pipe": p, "fsdp": f}

    barrier = pltpu.get_barrier_semaphore()
    partners = [
        (before, member),
        (before, flipped),
        (behind, member),
        (behind, flipped),
        (stages - 1 - pipe, member),
    ]
    partners += [(pipe, (member + i) % members) for i in range(1, members)]
    for p, f in partners:
        pl.semaphore_signal(barrier, inc=1, device_id=device(p, f), device_id_type=MESH)

    def weight_copy(i):
        part = pl.ds(pl.multiple_of(i * local, local), local)
        return pltpu.make_async_copy(
            weight_hbm.at[:, part], weight.at[:, part], weight_sem.at[i]
        )

    @pl.loop(0, members)
    def _(i):
        weight_copy(i).start()

    own_up = pltpu.make_async_copy(up_hbm, up.at[member], up_sem)
    own_up.start()

    routes = {
        NEAR: (shard, before, member),
        ACROSS: (shard, before, flipped),
        RIGHT0: (x_ref.at[NEAR], pipe, to_left),
        LEFT0: (x_ref.at[NEAR], pipe, to_right),
        RIGHT1: (x_ref.at[ACROSS], pipe, to_left),
        LEFT1: (x_ref.at[ACROSS], pipe, to_right),
        FAR0: (x_ref.at[LEFT0], pipe, to_right),
        FAR1: (x_ref.at[RIGHT1], pipe, to_left),
    }

    def columns(c):
        return pl.ds(pl.multiple_of(c * wide, wide), wide)

    def hop(slot, c):
        source, p, f = routes[slot]
        return pltpu.make_async_remote_copy(
            src_ref=source.at[:, columns(c)],
            dst_ref=x_ref.at[slot, :, columns(c)],
            send_sem=shard_send.at[slot, c],
            recv_sem=shard_recv.at[slot, c],
            device_id=device(p, f),
            device_id_type=MESH,
        )

    def up_copy(i):
        return pltpu.make_async_remote_copy(
            src_ref=up_hbm,
            dst_ref=up.at[member],
            send_sem=up_send.at[i - 1],
            recv_sem=up_recv.at[i - 1],
            device_id=device(pipe, (member + i) % members),
            device_id_type=MESH,
        )

    parked = [
        pltpu.make_async_remote_copy(
            src_ref=source,
            dst_ref=target,
            send_sem=parked_send.at[i],
            recv_sem=parked_recv.at[i],
            device_id=device(stages - 1 - pipe, member),
            device_id_type=MESH,
        )
        for i, (source, target) in enumerate(
            [(key_hbm, key), (value_hbm, value), (query_hbm, query)]
        )
    ]

    def rank_copy(i):
        peer = flipped if i == 0 else plane * ring + (x + i) % ring
        return pltpu.make_async_remote_copy(
            src_ref=rank_sum.at[1 if i == 0 else 0],
            dst_ref=rank_parts.at[i],
            send_sem=rank_send.at[i],
            recv_sem=rank_recv.at[i],
            device_id=device(pipe, peer),
            device_id_type=MESH,
        )

    pl.semaphore_wait(barrier, len(partners))

    @pl.loop(0, CHUNKS)
    def _(c):
        hop(NEAR, c).start()

    for i in range(1, members):
        up_copy(i).start()

    ids = jnp.broadcast_to(segments[...].astype(F32), (8, tokens))
    doc[...] = ids.T

    @pl.loop(0, CHUNKS)
    def _(c):
        hop(NEAR, c).wait_recv()
        hop(RIGHT0, c).start()
        hop(LEFT0, c).start()

    @pl.loop(0, CHUNKS)
    def _(c):
        hop(ACROSS, c).start()

    def relay(c):
        hop(LEFT0, c).wait_recv()
        hop(FAR0, c).start()
        hop(ACROSS, c).wait_recv()
        hop(RIGHT1, c).start()
        hop(LEFT1, c).start()

    relay(0)
    for copy in parked:
        copy.start()
    pl.loop(1, CHUNKS)(relay)

    def block_of(slot):
        side = (plane + slot) % 2
        return side * ring + (x + slot // 2) % ring

    def project_chunk(group, c):
        rows_in = jnp.concatenate(
            [x_ref[2 * group, :, columns(c)], x_ref[2 * group + 1, :, columns(c)]], axis=0
        )
        up_rows = [up[members // CHUNKS * c + i] for i in range(members // CHUNKS)]
        acc[...] += dot(weight[:, columns(c)], rows_in, NT)
        rank_acc[...] += dot(jnp.concatenate(up_rows, axis=1), rows_in, NT)

    def project_start():
        acc[...] = jnp.zeros_like(acc)
        rank_acc[...] = jnp.zeros_like(rank_acc)

    def project_end(group):
        projected = dot(down[...].astype(F32), rank_acc[...], TN, HIGHEST)
        total = (acc[...] + LORA_SCALE * projected).T.astype(BF16)
        ranked = rank_acc[...].T
        for i in range(2):
            gradient[2 * group + i] = total[i * rows : (i + 1) * rows]
            rank[2 * group + i] = ranked[i * rows : (i + 1) * rows]

    def project(group):
        project_start()
        pl.loop(0, CHUNKS)(functools.partial(project_chunk, group))
        project_end(group)

    own_up.wait()
    for i in range(1, members):
        up_copy(i).wait_recv()

    @pl.loop(0, members)
    def _(i):
        weight_copy(i).wait()

    project(NEAR // 2)

    @pl.loop(0, CHUNKS)
    def _(c):
        hop(RIGHT1, c).wait_recv()
        hop(FAR1, c).start()

    def arrived(slot):
        @pl.loop(0, CHUNKS)
        def _(c):
            hop(slot, c).wait_recv()

    arrived(RIGHT0)
    project(RIGHT0 // 2)
    arrived(LEFT1)
    project(LEFT0 // 2)

    def token_rows(block):
        return pl.ds(pl.multiple_of(block * rows, 32), rows)

    def key_window(block):
        begin = (block // (KEYS // rows)) * (block * rows + rows - KEYS)
        return pl.multiple_of(begin, 32)

    def allowed_keys(block, begin):
        lane = lax.broadcasted_iota(jnp.int32, (rows, lanes), 1) % rows
        spread = (lax.broadcasted_iota(jnp.int32, (rows, lanes), 0) == lane).astype(F32)
        own = dot(doc[token_rows(block), :], spread, TN)[0:1]
        other = doc[pl.ds(begin, KEYS), 0:1]
        place = block * rows + lane[0:1]
        position = begin + lax.broadcasted_iota(jnp.int32, (KEYS, lanes), 0)
        return (position <= place) & (other == own)

    def scores_of(block, begin):
        queries = stack_heads(query[token_rows(block), :])
        scores = dot(key[pl.ds(begin, KEYS), :], queries, NT) * (LOG2E / math.sqrt(HEAD))
        return queries, scores

    for copy in parked:
        copy.wait_recv()

    @pl.loop(0, members)
    def _(block):
        begin = key_window(block)
        _, scores = scores_of(block, begin)
        scores = jnp.where(allowed_keys(block, begin), scores, NEG)
        top = jnp.max(scores, axis=0, keepdims=True)
        expanded = jnp.exp2(scores - top)
        total = jnp.sum(expanded, axis=0, keepdims=True)
        probs = (expanded / total).astype(BF16)
        mixed = dot(value[pl.ds(begin, KEYS), :], probs, TN)
        mixed = unstack_heads(mixed.T.astype(BF16), rows)
        context[token_rows(block), :] = mixed
        lse[block] = top + jnp.log2(total)
        rank_context[token_rows(block), :] = dot(mixed, down[...], NT)

    rank_sum[0] = rank_context[...].T
    for i in range(1, ring):
        rank_copy(i).start()

    dk[...] = jnp.zeros_like(dk)
    dv[...] = jnp.zeros_like(dv)
    down_map_ref[...] = jnp.zeros_like(down_map_ref)
    up_map_ref[...] = jnp.zeros_like(up_map_ref)

    def dq_copy(slot):
        block = block_of(slot)
        return pltpu.make_async_copy(
            dq.at[token_rows(block), :], dq_ref.at[token_rows(block), :], dq_sem.at[slot]
        )

    def backward(slot):
        block = block_of(slot)
        begin = key_window(block)
        window = pl.ds(begin, KEYS)
        queries, scores = scores_of(block, begin)
        arriving = stack_heads(gradient[slot])
        mixed = context[token_rows(block), :]
        products = arriving.astype(F32) * stack_heads(mixed).astype(F32)
        delta = dot(jnp.ones((8, HEAD), F32), products, NT, HIGHEST)[0:1]
        shifted = jnp.where(allowed_keys(block, begin), scores - lse[block], NEG)
        probs = jnp.exp2(shifted)
        grad_probs = dot(value[window, :], arriving, NT)
        grad_scores = (probs * (grad_probs - delta)).astype(BF16)
        dv[window, :] += dot(probs.astype(BF16), arriving, NN)
        dk[window, :] += dot(grad_scores, queries, NN)
        grad_query = dot(key[window, :], grad_scores, TN) * (1.0 / math.sqrt(HEAD))
        dq[token_rows(block), :] = unstack_heads(grad_query.T.astype(BF16), rows)
        down_map_ref[...] += dot(rank[slot], mixed.astype(F32), TN, HIGHEST)
        dq_copy(slot).start()

    def up_map(slot):
        part = x_ref[slot, :, pl.ds(pl.multiple_of(member * local, local), local)]
        ranked = rank_context[token_rows(block_of(slot)), :]
        up_map_ref[...] += dot(ranked, part.astype(F32), TN, HIGHEST)

    pl.loop(NEAR, ACROSS + 1)(backward)
    for i in range(1, ring):
        rank_copy(i).wait_recv()
    rank_sum[1] = rank_sum[0] + rank_parts[1] + rank_parts[2] + rank_parts[3]
    rank_copy(0).start()
    pl.loop(RIGHT0, RIGHT1 + 1)(backward)
    pl.loop(LEFT0, LEFT1 + 1)(backward)
    rank_copy(0).wait_recv()
    rank_context[...] = (rank_sum[1] + rank_parts[0]).T
    pl.loop(NEAR, RIGHT1 + 1)(up_map)
    pl.loop(LEFT0, LEFT1 + 1)(up_map)

    project_start()

    @pl.loop(0, CHUNKS)
    def _(c):
        hop(FAR0, c).wait_recv()
        hop(FAR1, c).wait_recv()
        project_chunk(FAR0 // 2, c)

    project_end(FAR0 // 2)
    pl.loop(FAR0, FAR1 + 1)(backward)
    pl.loop(FAR0, FAR1 + 1)(up_map)

    dk_ref[...] = (dk[...] * (1.0 / math.sqrt(HEAD))).astype(BF16)
    dv_ref[...] = dv[...].astype(BF16)
    scale = LORA_SCALE / math.sqrt(tokens)
    down_map_ref[...] = down_map_ref[...] * scale
    up_map_ref[...] = up_map_ref[...] * scale

    for slot in range(members):

        @pl.loop(0, CHUNKS)
        def _(c):
            hop(slot, c).wait_send()

        dq_copy(slot).wait()
    for copy in parked:
        copy.wait_send()
    for i in range(1, members):
        up_copy(i).wait_send()
    for i in range(ring):
        rank_copy(i).wait_send()


def per_device(
    handoff_gradient,
    output_weight,
    adapter_down,
    adapter_up,
    stored_queries,
    stored_keys,
    stored_values,
    segments,
):
    stages = lax.axis_size("pipe")
    members = lax.axis_size("fsdp")
    rows, depth = handoff_gradient.shape[1:]
    tokens, width = stored_queries.shape[1:]
    ranks = adapter_down.shape[1]
    local = adapter_up.shape[2]
    lanes = width // HEAD * rows
    anywhere = pl.BlockSpec(memory_space=pl.ANY)
    on_chip = pl.BlockSpec(memory_space=pltpu.VMEM)
    dma = pltpu.SemaphoreType.DMA
    outputs = pl.pallas_call(
        functools.partial(kernel, stages, members),
        in_specs=[anywhere, anywhere, on_chip, anywhere, anywhere, anywhere, anywhere, on_chip],
        out_specs=[anywhere, on_chip, on_chip, on_chip, on_chip],
        out_shape=[
            jax.ShapeDtypeStruct((tokens, width), BF16),
            jax.ShapeDtypeStruct((tokens, HEAD), BF16),
            jax.ShapeDtypeStruct((tokens, HEAD), BF16),
            jax.ShapeDtypeStruct((ranks, width), F32),
            jax.ShapeDtypeStruct((ranks, local), F32),
        ],
        scratch_shapes=[
            pltpu.VMEM((members, rows, depth), BF16),
            pltpu.VMEM((width, depth), BF16),
            pltpu.VMEM((members, ranks, local), BF16),
            pltpu.VMEM((tokens, width), BF16),
            pltpu.VMEM((tokens, HEAD), BF16),
            pltpu.VMEM((tokens, HEAD), BF16),
            pltpu.VMEM((tokens, 8), F32),
            pltpu.VMEM((tokens, width), BF16),
            pltpu.VMEM((members, 1, lanes), F32),
            pltpu.VMEM((members, rows, width), BF16),
            pltpu.VMEM((members, rows, ranks), F32),
            pltpu.VMEM((width, 2 * rows), F32),
            pltpu.VMEM((ranks, 2 * rows), F32),
            pltpu.VMEM((tokens, width), BF16),
            pltpu.VMEM((tokens, HEAD), F32),
            pltpu.VMEM((tokens, HEAD), F32),
            pltpu.VMEM((tokens, ranks), F32),
            pltpu.VMEM((2, ranks, tokens), F32),
            pltpu.VMEM((4, ranks, tokens), F32),
            dma((members, CHUNKS)),
            dma((members, CHUNKS)),
            dma((3,)),
            dma((3,)),
            dma((members - 1,)),
            dma((members - 1,)),
            dma((4,)),
            dma((4,)),
            dma((members,)),
            dma,
            dma((members,)),
        ],
        compiler_params=pltpu.CompilerParams(
            collective_id=0, has_side_effects=True, vmem_limit_bytes=VMEM_BYTES
        ),
        name="relay",
    )(
        handoff_gradient[0],
        output_weight[0],
        adapter_down[0],
        adapter_up[0],
        stored_queries[0],
        stored_keys[0],
        stored_values[0],
        segments,
    )
    return tuple(output[None] for output in outputs)


def solution(mesh):
    split = P("pipe", None, "fsdp")
    rows = P("pipe", "fsdp", None)
    return jax.shard_map(
        per_device,
        mesh=mesh,
        in_specs=(rows, rows, split, split, split, split, split, P("pipe", None)),
        out_specs=(split,) * 5,
        check_vma=False,
    )
```

time: 606 us -> 167 us (0.28)
  waiting for transfers between devices: 410 us -> 0 us
  Pallas kernels: 0 us -> 161 us
  blocking collectives: 78.4 us -> 0 us
  matrix products: 63.8 us -> 0 us
  local copies, waits for them, and re-layouts: 21 us -> 5.35 us
  between operations: 14.2 us -> 0.68 us
  other arithmetic: 7.65 us -> 0 us
  starting transfers between devices: 7.47 us -> 0 us
    ppermute x5 -> x0, waiting for transfers between devices: 257 us -> none  [the longest x4 257 us: swapped(): return lax.ppermute(block, axis, route)]
    pallas_call x0 -> x1, Pallas kernels: none -> 161 us  [per_device(): pl.pallas_call(functools.partial(kernel, stages, members), in_specs=[anyw...]
    all_gather x1 -> x0, waiting for transfers between devices: 152 us -> none  [per_device(): lax.all_gather(handoff_gradient[0], 'fsdp', axis=0, tiled=True)]
    psum x2 -> x0, blocking collectives: 78.4 us -> none  [the longest x1 39.7 us: per_device(): rank_gradient = lax.psum(rank_portion, 'fsdp')]
    dot_general x24 -> x0, matrix products: 63.8 us -> none  [the longest x1 21.7 us: per_device(): jnp.einsum('td,qd->tq', incoming_gradient, output_weight[0], preferred_el...]
    ppermute x5 -> x0, starting transfers between devices: 7.43 us -> none  [the longest x4 5.56 us: swapped(): return lax.ppermute(block, axis, route)]
  transfers between devices with their start and end apart: 6 -> 0, of which waited for: 5 -> 0; matrix products, arithmetic and copies ran while one was open for 1% -> 0% of each run, Pallas kernels for 0% -> 0%
where the time goes in v3:
time: 167 us
  Pallas kernels  161 us (96%)
  local copies, waits for them, and re-layouts  5.35 us (3%)
    pallas_call x1, Pallas kernels, per_device(): pl.pallas_call(functools.partial(kernel, stages, members), in_specs=[anyw...  161 us
    unnamed x13, local copies, waits for them, and re-layouts  5.35 us

profile of v3, /device:TPU:0, one launch (start us, length us, event | category | flops | bytes accessed | tf_op | source)
XLA Modules:
  0.0 166.9 jit_solution(7588831756825710501)
XLA Ops:
  0.6 160.9 %relay.1 = (bf16[768,1024]{1,0:T(8,128)(2,1)}, bf16[768,128]{1,0:T(8,128)(2,1)}, bf16[768,128]{1,0:T(8,128)(2,1)}, f32[16,1024]{1,0:T(8,128)}, f32[16,1024]{1,0:T(8,128)}) custom-call(bf16[96,8192]{1,0:T(8,128)(2,1)} %bitcast.14, bf16[1024,8192]{1,0:T(8,128)(2,1)} %bitcast.12, bf16[16,1024]{1,0:T(8,128)(2,1)} %bitcast.22, bf16[16,1024]{1,0:T(8,128)(2,1)} %bitcast.23, ...), custom_call_target="tpu_custom_call" | custom-call | tf_op jit(solution)/shard_map/relay/pallas_call | solution.py:428
  161.5 0.0 copy-start.1
  161.5 0.0 copy-start
  161.6 0.0 copy-start.3
  161.6 0.0 copy-start.2
  161.6 2.7 %copy.18 = bf16[1,768,1024]{2,1,0:T(8,128)(2,1)} copy(bf16[1,768,1024]{2,1,0:T(8,128)(2,1)} %bitcast.13) | data formatting | bytes 3145728
  164.3 0.0 copy-done.1
  164.3 0.7 copy.19
  165.0 0.0 copy-done
  165.0 0.7 copy.20
  165.7 0.0 copy-done.3
  165.7 0.6 copy.21
  166.3 0.0 copy-done.2
  166.3 0.6 copy.22
Async XLA Ops:
  161.5 2.8 %copy-start.1 = (bf16[768,128]{1,0:T(8,128)(2,1)S(1)}, bf16[768,128]{1,0:T(8,128)(2,1)}, u32[]{:S(2)}) copy-start(bf16[768,128]{1,0:T(8,128)(2,1)} %get-tuple-element.11) | copy-start | bytes 589828
  161.5 3.4 %copy-start = (bf16[768,128]{1,0:T(8,128)(2,1)S(1)}, bf16[768,128]{1,0:T(8,128)(2,1)}, u32[]{:S(2)}) copy-start(bf16[768,128]{1,0:T(8,128)(2,1)} %get-tuple-element.12) | copy-start | bytes 589828
  161.6 4.1 %copy-start.3 = (f32[16,1024]{1,0:T(8,128)S(1)}, f32[16,1024]{1,0:T(8,128)}, u32[]{:S(2)}) copy-start(f32[16,1024]{1,0:T(8,128)} %get-tuple-element.13) | copy-start | bytes 196612
  161.6 4.7 %copy-start.2 = (f32[16,1024]{1,0:T(8,128)S(1)}, f32[16,1024]{1,0:T(8,128)}, u32[]{:S(2)}) copy-start(f32[16,1024]{1,0:T(8,128)} %get-tuple-element.14) | copy-start | bytes 196612

commit v4 on v3

--- a/solution.py
+++ b/solution.py
@@ -141,14 +141,18 @@
         RIGHT1: (x_ref.at[ACROSS], pipe, to_left),
         LEFT1: (x_ref.at[ACROSS], pipe, to_right),
         FAR0: (x_ref.at[LEFT0], pipe, to_right),
+        FAR1: (x_ref.at[LEFT1], pipe, to_right),
+    }
+    mirrored = {
+        FAR0: (x_ref.at[RIGHT0], pipe, to_left),
         FAR1: (x_ref.at[RIGHT1], pipe, to_left),
     }
 
     def columns(c):
         return pl.ds(pl.multiple_of(c * wide, wide), wide)
 
-    def hop(slot, c):
-        source, p, f = routes[slot]
+    def hop(slot, c, table=routes):
+        source, p, f = table[slot]
         return pltpu.make_async_remote_copy(
             src_ref=source.at[:, columns(c)],
             dst_ref=x_ref.at[slot, :, columns(c)],
@@ -195,10 +199,18 @@
 
     pl.semaphore_wait(barrier, len(partners))
 
+    even = pipe % 2 == 0
+
     @pl.loop(0, CHUNKS)
     def _(c):
         hop(NEAR, c).start()
 
+    def send_across():
+        @pl.loop(0, CHUNKS)
+        def _(c):
+            hop(ACROSS, c).start()
+
+    pl.when(even)(send_across)
     for i in range(1, members):
         up_copy(i).start()
 
@@ -211,50 +223,67 @@
         hop(RIGHT0, c).start()
         hop(LEFT0, c).start()
 
-    @pl.loop(0, CHUNKS)
-    def _(c):
-        hop(ACROSS, c).start()
-
-    def relay(c):
-        hop(LEFT0, c).wait_recv()
-        hop(FAR0, c).start()
-        hop(ACROSS, c).wait_recv()
-        hop(RIGHT1, c).start()
-        hop(LEFT1, c).start()
-
-    relay(0)
-    for copy in parked:
-        copy.start()
-    pl.loop(1, CHUNKS)(relay)
+    def relay_across():
+        @pl.loop(0, CHUNKS)
+        def _(c):
+            hop(ACROSS, c).wait_recv()
+            hop(RIGHT1, c).start()
+            hop(LEFT1, c).start()
+
+    def relay_far(far, left, right, c):
+        hop(left, c).wait_recv()
+        hop(far, c).start()
+        hop(right, c + 1).wait_recv()
+        hop(far, c + 1, mirrored).start()
+
+    def send_parked():
+        for copy in parked:
+            copy.start()
+
+    def relay_far_all(far, left, right):
+        @pl.loop(0, CHUNKS, step=2)
+        def _(c):
+            relay_far(far, left, right, c)
+
+    odd = pipe % 2 == 1
+
+    @pl.when(even)
+    def _():
+        relay_far_all(FAR0, LEFT0, RIGHT0)
+        send_parked()
+
+    @pl.when(odd)
+    def _():
+        send_across()
+        send_parked()
+        relay_across()
+        relay_far_all(FAR0, LEFT0, RIGHT0)
 
     def block_of(slot):
         side = (plane + slot) % 2
         return side * ring + (x + slot // 2) % ring
 
-    def project_chunk(group, c):
-        rows_in = jnp.concatenate(
-            [x_ref[2 * group, :, columns(c)], x_ref[2 * group + 1, :, columns(c)]], axis=0
-        )
+    def project_chunk(slots, c):
+        used = pl.ds(0, len(slots) * rows)
+        rows_in = jnp.concatenate([x_ref[slot, :, columns(c)] for slot in slots], axis=0)
         up_rows = [up[members // CHUNKS * c + i] for i in range(members // CHUNKS)]
-        acc[...] += dot(weight[:, columns(c)], rows_in, NT)
-        rank_acc[...] += dot(jnp.concatenate(up_rows, axis=1), rows_in, NT)
+        product = dot(weight[:, columns(c)], rows_in, NT)
+        ranked = dot(jnp.concatenate(up_rows, axis=1), rows_in, NT)
+        acc[:, used] = acc[:, used] + product
+        rank_acc[:, used] = rank_acc[:, used] + ranked
 
     def project_start():
         acc[...] = jnp.zeros_like(acc)
         rank_acc[...] = jnp.zeros_like(rank_acc)
 
-    def project_end(group):
-        projected = dot(down[...].astype(F32), rank_acc[...], TN, HIGHEST)
-        total = (acc[...] + LORA_SCALE * projected).T.astype(BF16)
-        ranked = rank_acc[...].T
-        for i in range(2):
-            gradient[2 * group + i] = total[i * rows : (i + 1) * rows]
-            rank[2 * group + i] = ranked[i * rows : (i + 1) * rows]
-
-    def project(group):
-        project_start()
-        pl.loop(0, CHUNKS)(functools.partial(project_chunk, group))
-        project_end(group)
+    def project_end(slots):
+        used = pl.ds(0, len(slots) * rows)
+        projected = dot(down[...].astype(F32), rank_acc[:, used], TN, HIGHEST)
+        total = (acc[:, used] + LORA_SCALE * projected).T.astype(BF16)
+        ranked = rank_acc[:, used].T
+        for i, slot in enumerate(slots):
+            gradient[slot] = total[i * rows : (i + 1) * rows]
+            rank[slot] = ranked[i * rows : (i + 1) * rows]
 
     own_up.wait()
     for i in range(1, members):
@@ -264,22 +293,27 @@
     def _(i):
         weight_copy(i).wait()
 
-    project(NEAR // 2)
-
-    @pl.loop(0, CHUNKS)
+    own = (NEAR, RIGHT0, FAR0, LEFT0)
+    project_start()
+
+    @pl.loop(0, CHUNKS, step=2)
     def _(c):
-        hop(RIGHT1, c).wait_recv()
-        hop(FAR1, c).start()
-
-    def arrived(slot):
-        @pl.loop(0, CHUNKS)
-        def _(c):
-            hop(slot, c).wait_recv()
-
-    arrived(RIGHT0)
-    project(RIGHT0 // 2)
-    arrived(LEFT1)
-    project(LEFT0 // 2)
+        hop(RIGHT0, c).wait_recv()
+        hop(FAR0, c).wait_recv()
+        project_chunk(own, c)
+        hop(LEFT0, c + 1).wait_recv()
+        hop(FAR0, c + 1).wait_recv()
+        project_chunk(own, c + 1)
+
+    project_end(own)
+
+    @pl.when(even)
+    def _():
+        relay_across()
+
+    @pl.when(odd)
+    def _():
+        relay_far_all(FAR1, LEFT1, RIGHT1)
 
     def token_rows(block):
         return pl.ds(pl.multiple_of(block * rows, 32), rows)
@@ -288,37 +322,42 @@
         begin = (block // (KEYS // rows)) * (block * rows + rows - KEYS)
         return pl.multiple_of(begin, 32)
 
-    def allowed_keys(block, begin):
+    def allowed_keys(block, begin, reach=KEYS):
         lane = lax.broadcasted_iota(jnp.int32, (rows, lanes), 1) % rows
         spread = (lax.broadcasted_iota(jnp.int32, (rows, lanes), 0) == lane).astype(F32)
         own = dot(doc[token_rows(block), :], spread, TN)[0:1]
-        other = doc[pl.ds(begin, KEYS), 0:1]
+        other = doc[pl.ds(begin, reach), 0:1]
         place = block * rows + lane[0:1]
-        position = begin + lax.broadcasted_iota(jnp.int32, (KEYS, lanes), 0)
+        position = begin + lax.broadcasted_iota(jnp.int32, (reach, lanes), 0)
         return (position <= place) & (other == own)
 
-    def scores_of(block, begin):
+    def scores_of(block, begin, reach=KEYS):
         queries = stack_heads(query[token_rows(block), :])
-        scores = dot(key[pl.ds(begin, KEYS), :], queries, NT) * (LOG2E / math.sqrt(HEAD))
+        scores = dot(key[pl.ds(begin, reach), :], queries, NT) * (LOG2E / math.sqrt(HEAD))
         return queries, scores
 
     for copy in parked:
         copy.wait_recv()
 
-    @pl.loop(0, members)
-    def _(block):
+    def forward(reach, block):
         begin = key_window(block)
-        _, scores = scores_of(block, begin)
-        scores = jnp.where(allowed_keys(block, begin), scores, NEG)
+        _, scores = scores_of(block, begin, reach)
+        scores = jnp.where(allowed_keys(block, begin, reach), scores, NEG)
         top = jnp.max(scores, axis=0, keepdims=True)
         expanded = jnp.exp2(scores - top)
         total = jnp.sum(expanded, axis=0, keepdims=True)
         probs = (expanded / total).astype(BF16)
-        mixed = dot(value[pl.ds(begin, KEYS), :], probs, TN)
+        mixed = dot(value[pl.ds(begin, reach), :], probs, TN)
         mixed = unstack_heads(mixed.T.astype(BF16), rows)
         context[token_rows(block), :] = mixed
         lse[block] = top + jnp.log2(total)
         rank_context[token_rows(block), :] = dot(mixed, down[...], NT)
+
+    done = 0
+    for reach in (KEYS // 2, 3 * KEYS // 4, KEYS):
+        until = members if reach == KEYS else reach // rows
+        pl.loop(done, until)(functools.partial(forward, reach))
+        done = until
 
     rank_sum[0] = rank_context[...].T
     for i in range(1, ring):
@@ -360,29 +399,43 @@
         ranked = rank_context[token_rows(block_of(slot)), :]
         up_map_ref[...] += dot(ranked, part.astype(F32), TN, HIGHEST)
 
-    pl.loop(NEAR, ACROSS + 1)(backward)
+    @pl.when(even)
+    def _():
+        relay_far_all(FAR1, LEFT1, RIGHT1)
+
+    pl.loop(NEAR, FAR0, step=2)(backward)
     for i in range(1, ring):
         rank_copy(i).wait_recv()
     rank_sum[1] = rank_sum[0] + rank_parts[1] + rank_parts[2] + rank_parts[3]
     rank_copy(0).start()
-    pl.loop(RIGHT0, RIGHT1 + 1)(backward)
-    pl.loop(LEFT0, LEFT1 + 1)(backward)
+    pl.loop(FAR0, members, step=2)(backward)
+    project_start()
+
+    @pl.loop(0, CHUNKS, step=2)
+    def _(c):
+        hop(RIGHT1, c).wait_recv()
+        project_chunk((ACROSS, RIGHT1), c)
+        project_chunk((ACROSS, RIGHT1), c + 1)
+
+    project_end((ACROSS, RIGHT1))
+    pl.loop(ACROSS, FAR1, step=2)(backward)
     rank_copy(0).wait_recv()
     rank_context[...] = (rank_sum[1] + rank_parts[0]).T
-    pl.loop(NEAR, RIGHT1 + 1)(up_map)
-    pl.loop(LEFT0, LEFT1 + 1)(up_map)
-
+    pl.loop(NEAR, FAR1)(up_map)
+    up_map(LEFT0)
     project_start()
 
-    @pl.loop(0, CHUNKS)
+    @pl.loop(0, CHUNKS, step=2)
     def _(c):
-        hop(FAR0, c).wait_recv()
         hop(FAR1, c).wait_recv()
-        project_chunk(FAR0 // 2, c)
-
-    project_end(FAR0 // 2)
-    pl.loop(FAR0, FAR1 + 1)(backward)
-    pl.loop(FAR0, FAR1 + 1)(up_map)
+        project_chunk((FAR1, LEFT1), c)
+        hop(LEFT1, c + 1).wait_recv()
+        hop(FAR1, c + 1).wait_recv()
+        project_chunk((FAR1, LEFT1), c + 1)
+
+    project_end((FAR1, LEFT1))
+    pl.loop(FAR1, members, step=2)(backward)
+    pl.loop(FAR1, members, step=2)(up_map)
 
     dk_ref[...] = (dk[...] * (1.0 / math.sqrt(HEAD))).astype(BF16)
     dv_ref[...] = dv[...].astype(BF16)
@@ -448,8 +501,8 @@
             pltpu.VMEM((members, 1, lanes), F32),
             pltpu.VMEM((members, rows, width), BF16),
             pltpu.VMEM((members, rows, ranks), F32),
-            pltpu.VMEM((width, 2 * rows), F32),
-            pltpu.VMEM((ranks, 2 * rows), F32),
+            pltpu.VMEM((width, 4 * rows), F32),
+            pltpu.VMEM((ranks, 4 * rows), F32),
             pltpu.VMEM((tokens, width), BF16),
             pltpu.VMEM((tokens, HEAD), F32),
             pltpu.VMEM((tokens, HEAD), F32),

time: 167 us -> 160 us (0.958)
  the two profiles are of different devices: /device:TPU:0 before, /device:TPU:25 now
where the time goes in v4:
time: 160 us; the launch traced here: 159 us
  Pallas kernels  153 us (96%)
  local copies, waits for them, and re-layouts  5.35 us (3%)
    pallas_call x1, Pallas kernels, per_device(): pl.pallas_call(functools.partial(kernel, stages, members), in_specs=[anyw...  153 us
    unnamed x13, local copies, waits for them, and re-layouts  5.35 us

profile of v4, /device:TPU:25, one launch (start us, length us, event | category | flops | bytes accessed | tf_op | source)
XLA Modules:
  0.0 159.4 jit_solution(9292071209150126072)
XLA Ops:
  0.6 153.4 %relay.1 = (bf16[768,1024]{1,0:T(8,128)(2,1)}, bf16[768,128]{1,0:T(8,128)(2,1)}, bf16[768,128]{1,0:T(8,128)(2,1)}, f32[16,1024]{1,0:T(8,128)}, f32[16,1024]{1,0:T(8,128)}) custom-call(bf16[96,8192]{1,0:T(8,128)(2,1)} %bitcast.14, bf16[1024,8192]{1,0:T(8,128)(2,1)} %bitcast.12, bf16[16,1024]{1,0:T(8,128)(2,1)} %bitcast.22, bf16[16,1024]{1,0:T(8,128)(2,1)} %bitcast.23, ...), custom_call_target="tpu_custom_call" | custom-call | tf_op jit(solution)/shard_map/relay/pallas_call | solution.py:481
  154.0 0.0 copy-start.1
  154.0 0.0 copy-start
  154.0 0.0 copy-start.3
  154.0 0.0 copy-start.2
  154.0 2.7 %copy.18 = bf16[1,768,1024]{2,1,0:T(8,128)(2,1)} copy(bf16[1,768,1024]{2,1,0:T(8,128)(2,1)} %bitcast.13) | data formatting | bytes 3145728
  156.8 0.0 copy-done.1
  156.8 0.7 copy.19
  157.5 0.0 copy-done
  157.5 0.7 copy.20
  158.1 0.0 copy-done.3
  158.1 0.6 copy.21
  158.8 0.0 copy-done.2
  158.8 0.6 copy.22
Async XLA Ops:
  154.0 2.8 %copy-start.1 = (bf16[768,128]{1,0:T(8,128)(2,1)S(1)}, bf16[768,128]{1,0:T(8,128)(2,1)}, u32[]{:S(2)}) copy-start(bf16[768,128]{1,0:T(8,128)(2,1)} %get-tuple-element.11) | copy-start | bytes 589828
  154.0 3.4 %copy-start = (bf16[768,128]{1,0:T(8,128)(2,1)S(1)}, bf16[768,128]{1,0:T(8,128)(2,1)}, u32[]{:S(2)}) copy-start(bf16[768,128]{1,0:T(8,128)(2,1)} %get-tuple-element.12) | copy-start | bytes 589828
  154.0 4.1 %copy-start.3 = (f32[16,1024]{1,0:T(8,128)S(1)}, f32[16,1024]{1,0:T(8,128)}, u32[]{:S(2)}) copy-start(f32[16,1024]{1,0:T(8,128)} %get-tuple-element.13) | copy-start | bytes 196612
  154.0 4.7 %copy-start.2 = (f32[16,1024]{1,0:T(8,128)S(1)}, f32[16,1024]{1,0:T(8,128)}, u32[]{:S(2)}) copy-start(f32[16,1024]{1,0:T(8,128)} %get-tuple-element.14) | copy-start | bytes 196612

commit v5 on v4

--- a/solution.py
+++ b/solution.py
@@ -29,6 +29,20 @@
 
 def dot(a, b, dims, precision=None):
     return lax.dot_general(a, b, dims, precision=precision, preferred_element_type=F32)
+
+
+def split(value, axis):
+    high = value.astype(BF16)
+    rest = value - high.astype(F32)
+    middle = rest.astype(BF16)
+    low = (rest - middle.astype(F32)).astype(BF16)
+    return jnp.concatenate([high, middle, low], axis=axis)
+
+
+def exact_tn(value, exact):
+    product = dot(split(value.T, 0), exact, NN)
+    count = product.shape[0] // 3
+    return product[:count] + product[count : 2 * count] + product[2 * count :]
 
 
 def stack_heads(rows):
@@ -278,7 +292,8 @@
 
     def project_end(slots):
         used = pl.ds(0, len(slots) * rows)
-        projected = dot(down[...].astype(F32), rank_acc[:, used], TN, HIGHEST)
+        thrice = jnp.concatenate([down[...]] * 3, axis=0)
+        projected = dot(thrice, split(rank_acc[:, used], 0), TN)
         total = (acc[:, used] + LORA_SCALE * projected).T.astype(BF16)
         ranked = rank_acc[:, used].T
         for i, slot in enumerate(slots):
@@ -382,7 +397,7 @@
         arriving = stack_heads(gradient[slot])
         mixed = context[token_rows(block), :]
         products = arriving.astype(F32) * stack_heads(mixed).astype(F32)
-        delta = dot(jnp.ones((8, HEAD), F32), products, NT, HIGHEST)[0:1]
+        delta = dot(jnp.ones((16, 3 * HEAD), BF16), split(products, 1), NT)[0:1]
         shifted = jnp.where(allowed_keys(block, begin), scores - lse[block], NEG)
         probs = jnp.exp2(shifted)
         grad_probs = dot(value[window, :], arriving, NT)
@@ -391,24 +406,19 @@
         dk[window, :] += dot(grad_scores, queries, NN)
         grad_query = dot(key[window, :], grad_scores, TN) * (1.0 / math.sqrt(HEAD))
         dq[token_rows(block), :] = unstack_heads(grad_query.T.astype(BF16), rows)
-        down_map_ref[...] += dot(rank[slot], mixed.astype(F32), TN, HIGHEST)
+        down_map_ref[...] += exact_tn(rank[slot], mixed)
         dq_copy(slot).start()
 
     def up_map(slot):
         part = x_ref[slot, :, pl.ds(pl.multiple_of(member * local, local), local)]
         ranked = rank_context[token_rows(block_of(slot)), :]
-        up_map_ref[...] += dot(ranked, part.astype(F32), TN, HIGHEST)
+        up_map_ref[...] += exact_tn(ranked, part)
 
     @pl.when(even)
     def _():
         relay_far_all(FAR1, LEFT1, RIGHT1)
 
-    pl.loop(NEAR, FAR0, step=2)(backward)
-    for i in range(1, ring):
-        rank_copy(i).wait_recv()
-    rank_sum[1] = rank_sum[0] + rank_parts[1] + rank_parts[2] + rank_parts[3]
-    rank_copy(0).start()
-    pl.loop(FAR0, members, step=2)(backward)
+    pl.loop(NEAR, members, step=2)(backward)
     project_start()
 
     @pl.loop(0, CHUNKS, step=2)
@@ -419,10 +429,10 @@
 
     project_end((ACROSS, RIGHT1))
     pl.loop(ACROSS, FAR1, step=2)(backward)
-    rank_copy(0).wait_recv()
-    rank_context[...] = (rank_sum[1] + rank_parts[0]).T
-    pl.loop(NEAR, FAR1)(up_map)
-    up_map(LEFT0)
+    for i in range(1, ring):
+        rank_copy(i).wait_recv()
+    rank_sum[1] = rank_sum[0] + rank_parts[1] + rank_parts[2] + rank_parts[3]
+    rank_copy(0).start()
     project_start()
 
     @pl.loop(0, CHUNKS, step=2)
@@ -435,13 +445,12 @@
 
     project_end((FAR1, LEFT1))
     pl.loop(FAR1, members, step=2)(backward)
-    pl.loop(FAR1, members, step=2)(up_map)
+    rank_copy(0).wait_recv()
+    rank_context[...] = (rank_sum[1] + rank_parts[0]).T
+    pl.loop(0, members)(up_map)
 
     dk_ref[...] = (dk[...] * (1.0 / math.sqrt(HEAD))).astype(BF16)
     dv_ref[...] = dv[...].astype(BF16)
-    scale = LORA_SCALE / math.sqrt(tokens)
-    down_map_ref[...] = down_map_ref[...] * scale
-    up_map_ref[...] = up_map_ref[...] * scale
 
     for slot in range(members):
 
@@ -456,6 +465,17 @@
         up_copy(i).wait_send()
     for i in range(ring):
         rank_copy(i).wait_send()
+
+
+def finish_kernel(scale, dq_in, dk_in, dv_in, down_map_in, up_map_in, dq, dk, dv, down_map, up_map):
+    dq[...] = dq_in[...]
+
+    @pl.when(pl.program_id(0) == 0)
+    def _():
+        dk[...] = dk_in[...]
+        dv[...] = dv_in[...]
+        down_map[...] = down_map_in[...] * scale
+        up_map[...] = up_map_in[...] * scale
 
 
 def per_device(
@@ -535,6 +555,18 @@
         stored_values[0],
         segments,
     )
+    pieces = 4
+    specs = [pl.BlockSpec((tokens // pieces, width), lambda i: (i, 0))]
+    specs += [pl.BlockSpec(output.shape, lambda i: (0, 0)) for output in outputs[1:]]
+    outputs = pl.pallas_call(
+        functools.partial(finish_kernel, LORA_SCALE / math.sqrt(tokens)),
+        grid=(pieces,),
+        in_specs=specs,
+        out_specs=specs,
+        out_shape=[jax.ShapeDtypeStruct(output.shape, output.dtype) for output in outputs],
+        compiler_params=pltpu.CompilerParams(vmem_limit_bytes=VMEM_BYTES),
+        name="finish",
+    )(*outputs)
     return tuple(output[None] for output in outputs)
 
 

time: 160 us -> 148 us (0.925)
  the two profiles are of different devices: /device:TPU:25 before, /device:TPU:0 now
where the time goes in v5:
time: 148 us; the launch traced here: 145 us
  Pallas kernels  144 us (97%)
    pallas_call x1, Pallas kernels, per_device(): pl.pallas_call(functools.partial(kernel, stages, members), in_specs=[anyw...  140 us
    pallas_call x1, Pallas kernels, per_device(): pl.pallas_call(functools.partial(finish_kernel, LORA_SCALE / math.sqrt(to...  3.94 us

profile of v5, /device:TPU:0, one launch (start us, length us, event | category | flops | bytes accessed | tf_op | source)
XLA Modules:
  0.0 144.6 jit_solution(8330352799099677506)
XLA Ops:
  0.6 139.9 %relay.1 = (bf16[768,1024]{1,0:T(8,128)(2,1)}, bf16[768,128]{1,0:T(8,128)(2,1)}, bf16[768,128]{1,0:T(8,128)(2,1)}, f32[16,1024]{1,0:T(8,128)}, f32[16,1024]{1,0:T(8,128)}) custom-call(bf16[96,8192]{1,0:T(8,128)(2,1)} %bitcast.13, bf16[1024,8192]{1,0:T(8,128)(2,1)} %bitcast.12, bf16[16,1024]{1,0:T(8,128)(2,1)} %bitcast.17, bf16[16,1024]{1,0:T(8,128)(2,1)} %bitcast.18, ...), custom_call_target="tpu_custom_call" | custom-call | tf_op jit(solution)/shard_map/relay/pallas_call | solution.py:501
  140.6 3.9 %finish.1 = (bf16[768,1024]{1,0:T(8,128)(2,1)}, bf16[768,128]{1,0:T(8,128)(2,1)}, bf16[768,128]{1,0:T(8,128)(2,1)}, f32[16,1024]{1,0:T(8,128)}, f32[16,1024]{1,0:T(8,128)}) custom-call(bf16[768,1024]{1,0:T(8,128)(2,1)} %get-tuple-element.15.dq_in, bf16[768,128]{1,0:T(8,128)(2,1)} %get-tuple-element.16.dk_in, bf16[768,128]{1,0:T(8,128)(2,1)} %get-tuple-element.17.dv_in, ...), custom_call_target="tpu_custom_call" | custom-call | tf_op jit(solution)/shard_map/finish/pallas_call | solution.py:561

commit v6 on v5

--- a/solution.py
+++ b/solution.py
@@ -94,6 +94,8 @@
     shard_recv,
     parked_send,
     parked_recv,
+    query_send,
+    query_recv,
     up_send,
     up_recv,
     rank_send,
@@ -196,9 +198,20 @@
             device_id_type=MESH,
         )
         for i, (source, target) in enumerate(
-            [(key_hbm, key), (value_hbm, value), (query_hbm, query)]
+            [(key_hbm, key), (value_hbm, value)]
         )
     ]
+
+    def query_copy(block):
+        part = pl.ds(pl.multiple_of(block * rows, 32), rows)
+        return pltpu.make_async_remote_copy(
+            src_ref=query_hbm.at[part, :],
+            dst_ref=query.at[part, :],
+            send_sem=query_send.at[block],
+            recv_sem=query_recv.at[block],
+            device_id=device(stages - 1 - pipe, member),
+            device_id_type=MESH,
+        )
 
     def rank_copy(i):
         peer = flipped if i == 0 else plane * ring + (x + i) % ring
@@ -254,6 +267,10 @@
         for copy in parked:
             copy.start()
 
+        @pl.loop(0, members)
+        def _(block):
+            query_copy(block).start()
+
     def relay_far_all(far, left, right):
         @pl.loop(0, CHUNKS, step=2)
         def _(c):
@@ -322,10 +339,6 @@
 
     project_end(own)
 
-    @pl.when(even)
-    def _():
-        relay_across()
-
     @pl.when(odd)
     def _():
         relay_far_all(FAR1, LEFT1, RIGHT1)
@@ -355,6 +368,7 @@
         copy.wait_recv()
 
     def forward(reach, block):
+        query_copy(block).wait_recv()
         begin = key_window(block)
         _, scores = scores_of(block, begin, reach)
         scores = jnp.where(allowed_keys(block, begin, reach), scores, NEG)
@@ -414,11 +428,14 @@
         ranked = rank_context[token_rows(block_of(slot)), :]
         up_map_ref[...] += exact_tn(ranked, part)
 
+    pl.when(even)(relay_across)
+    pl.loop(NEAR, FAR0, step=2)(backward)
+
     @pl.when(even)
     def _():
         relay_far_all(FAR1, LEFT1, RIGHT1)
 
-    pl.loop(NEAR, members, step=2)(backward)
+    pl.loop(FAR0, members, step=2)(backward)
     project_start()
 
     @pl.loop(0, CHUNKS, step=2)
@@ -459,6 +476,7 @@
             hop(slot, c).wait_send()
 
         dq_copy(slot).wait()
+        query_copy(slot).wait_send()
     for copy in parked:
         copy.wait_send()
     for i in range(1, members):
@@ -531,8 +549,10 @@
             pltpu.VMEM((4, ranks, tokens), F32),
             dma((members, CHUNKS)),
             dma((members, CHUNKS)),
-            dma((3,)),
-            dma((3,)),
+            dma((2,)),
+            dma((2,)),
+            dma((members,)),
+            dma((members,)),
             dma((members - 1,)),
             dma((members - 1,)),
             dma((4,)),

time: 148 us -> 142 us (0.959); the launches traced: 145 us -> 141 us
  Pallas kernels: 144 us -> 140 us
    pallas_call x1, Pallas kernels: 140 us -> 136 us  [per_device(): pl.pallas_call(functools.partial(kernel, stages, members), in_specs=[anyw...]
where the time goes in v6:
time: 142 us; the launch traced here: 141 us
  Pallas kernels  140 us (99%)
    pallas_call x1, Pallas kernels, per_device(): pl.pallas_call(functools.partial(kernel, stages, members), in_specs=[anyw...  136 us
    pallas_call x1, Pallas kernels, per_device(): pl.pallas_call(functools.partial(finish_kernel, LORA_SCALE / math.sqrt(to...  3.94 us

profile of v6, /device:TPU:0, one launch (start us, length us, event | category | flops | bytes accessed | tf_op | source)
XLA Modules:
  0.0 141.2 jit_solution(3176169170406518175)
XLA Ops:
  0.6 136.5 %relay.1 = (bf16[768,1024]{1,0:T(8,128)(2,1)}, bf16[768,128]{1,0:T(8,128)(2,1)}, bf16[768,128]{1,0:T(8,128)(2,1)}, f32[16,1024]{1,0:T(8,128)}, f32[16,1024]{1,0:T(8,128)}) custom-call(bf16[96,8192]{1,0:T(8,128)(2,1)} %bitcast.13, bf16[1024,8192]{1,0:T(8,128)(2,1)} %bitcast.12, bf16[16,1024]{1,0:T(8,128)(2,1)} %bitcast.17, bf16[16,1024]{1,0:T(8,128)(2,1)} %bitcast.18, ...), custom_call_target="tpu_custom_call" | custom-call | tf_op jit(solution)/shard_map/relay/pallas_call | solution.py:519
  137.1 3.9 %finish.1 = (bf16[768,1024]{1,0:T(8,128)(2,1)}, bf16[768,128]{1,0:T(8,128)(2,1)}, bf16[768,128]{1,0:T(8,128)(2,1)}, f32[16,1024]{1,0:T(8,128)}, f32[16,1024]{1,0:T(8,128)}) custom-call(bf16[768,1024]{1,0:T(8,128)(2,1)} %get-tuple-element.15.dq_in, bf16[768,128]{1,0:T(8,128)(2,1)} %get-tuple-element.16.dk_in, bf16[768,128]{1,0:T(8,128)(2,1)} %get-tuple-element.17.dv_in, ...), custom_call_target="tpu_custom_call" | custom-call | tf_op jit(solution)/shard_map/finish/pallas_call | solution.py:581
